TPU v7x, 256 devices: a whole 4x4x8 slice. The times are simulated.
256 devices in a mesh: rows: 128 (over z, x, y), half: 2 (over core).
Axes of the slice: x: 4, y: 4, z: 8, core: 2. Of those that a mesh axis runs over, the one named last changes fastest.
Arguments:
- source_feats: bfloat16 [131072, 1024], P('rows', 'half'), may hold values from -6 to 6
- rel_weight: bfloat16 [3, 2, 512, 512], P(None, 'half'), may hold values from -0.25 to 0.25
- tiles: bfloat16 [4096, 64, 512], P('rows'), may hold values from -0.25 to 0.25
- src_blk: int32 [4096, 8], P('rows'), may hold values from 0 to 15
- rel_id: int32 [4096, 8], P('rows'), may hold values from 0 to 2
- owner: int32 [4096, 1], P('rows'), may hold values from 0 to 127; in each aligned block of 32 rows (0 to 31, 32 to 63, ...) at most 2 rows name the same one
- local_blk: int32 [4096], P('rows'), may hold values from 0 to 31
- in_degree: int32 [262144], P('rows'), may hold values from 1 to 16
- mix_weight: bfloat16 [1024, 1024], P(None, 'half'), may hold values from -0.1875 to 0.1875
- bias: float32 [1024], P('half'), may hold values from -0.5 to 0.5
Outputs:
- out: bfloat16 [262144, 1024], P('rows', 'half')
Inputs may be any that keep to these rules, and one draw needn't show every extreme that they name: Among the 32 rows held by one device along rows, no owner is named more than 2 times, some owner exactly 2 times, and every owner is named somewhere.
All inputs are finite; a program needn't handle non-finite values.
Results may differ from a plain program's by a relative error of at most 0.0054.
Values may be sent and summed in bfloat16 or wider, within the bound.
A program may use at most 128 MiB of HBM per device.

v0:
```python
import jax
import jax.numpy as jnp
from jax import lax
from jax.sharding import PartitionSpec as P


def local(
    source_feats, rel_weight, tiles, src_blk, rel_id, owner, local_blk, in_degree, mix_weight, bias
):
    n_rows = lax.axis_size("rows")
    src_dev, half_w = source_feats.shape
    tile = tiles.shape[1]
    parts, per_row = src_blk.shape
    n_rel = rel_weight.shape[0]
    n_src_blocks = src_dev // tile
    n_blocks = n_rel * n_src_blocks
    n_local = in_degree.shape[0] // tile
    capacity = max(2, 2 * parts // n_rows)
    msgs = jnp.einsum(
        "sj,rjc->rsc", source_feats, rel_weight[:, 0], preferred_element_type=jnp.float32
    ).astype(jnp.bfloat16)
    flat_blocks = msgs.reshape(n_blocks, tile * half_w)
    picks = rel_id * n_src_blocks + src_blk
    per_turn = 16
    block_ids = jnp.arange(n_blocks, dtype=jnp.int32)

    def partial_group(operands):
        group_tiles, group_picks = operands
        chooser = (group_picks.reshape(per_turn * per_row)[:, None] == block_ids[None, :]).astype(
            jnp.bfloat16
        )
        picked = jnp.dot(chooser, flat_blocks, preferred_element_type=jnp.float32).astype(
            jnp.bfloat16
        )
        picked = picked.reshape(per_turn, per_row * tile, half_w)
        return jnp.einsum(
            "pim,pmc->pic", group_tiles, picked, preferred_element_type=jnp.float32
        ).astype(jnp.bfloat16)

    grouped = (
        tiles.reshape(parts // per_turn, per_turn, tile, per_row * tile),
        picks.reshape(parts // per_turn, per_turn, per_row),
    )
    partials = lax.map(partial_group, grouped).reshape(parts, tile * half_w)
    target_dev = owner[:, 0]
    positions = jnp.arange(parts, dtype=jnp.int32)
    earlier = (target_dev[:, None] == target_dev[None, :]) & (
        positions[None, :] < positions[:, None]
    )
    rank = jnp.sum(earlier.astype(jnp.int32), axis=1)
    slot = target_dev * capacity + rank
    slot_ids = jnp.arange(n_rows * capacity, dtype=jnp.int32)
    placing = slot_ids[:, None] == slot[None, :]
    outgoing = jnp.dot(
        placing.astype(jnp.bfloat16), partials, preferred_element_type=jnp.float32
    ).astype(jnp.bfloat16)
    out_ids = jnp.sum(jnp.where(placing, local_blk[None, :] + 1, 0), axis=1) - 1
    block_index = jnp.arange(n_local, dtype=jnp.int32)
    arrived, arrived_ids = (
        lax.all_to_all(outgoing, "rows", split_axis=0, concat_axis=0, tiled=True),
        lax.all_to_all(out_ids, "rows", split_axis=0, concat_axis=0, tiled=True),
    )
    selector = (arrived_ids[None, :] == block_index[:, None]).astype(jnp.bfloat16)
    summed = jnp.dot(selector, arrived, preferred_element_type=jnp.float32)
    summed = summed.reshape(n_local * tile, half_w)
    agg = (summed / in_degree.astype(jnp.float32)[:, None]).astype(jnp.bfloat16)
    mixed = jnp.dot(
        lax.all_gather(agg, "half", axis=1, tiled=True),
        mix_weight,
        preferred_element_type=jnp.float32,
    )
    return jax.nn.relu(mixed + bias).astype(jnp.bfloat16)


def solution(mesh):
    placed = (
        P("rows", "half"),
        P(None, "half", None, None),
        P("rows", None, None),
        P("rows", None),
        P("rows", None),
        P("rows", None),
        P("rows"),
        P("rows"),
        P(None, "half"),
        P("half"),
    )
    return jax.shard_map(
        local, mesh=mesh, in_specs=placed, out_specs=P("rows", "half"), check_vma=False
    )
```

profile of v0, /device:TPU:1, one launch (start us, length us, event | category | flops | bytes accessed | tf_op | source)
XLA Modules:
  0.0 598.6 jit_solution(10182642154321596765)
XLA Ops:
  6.5 1.0 convert_reduce_fusion
  7.5 0.7 multiply_add_fusion.1
  8.2 0.1 select_reduce_fusion
  8.3 0.8 sub.7
  9.0 16.3 %all-to-all-start = ((s32[128,2,1]{1,2,0:T(1,128)}), s32[128,2,1]{1,2,0:T(1,128)S(1)}, u32[]{:S(2)}, u32[]{:S(2)}) async-start(s32[128,2,1]{1,2,0:T(1,128)} %bitcast.1), calls=%async_computation | async-start | bytes 131072 | tf_op jit(solution)/shard_map/all_to_all | solution.py:61
  25.4 4.8 convert_bitcast_fusion
  30.2 4.7 copy.23
  34.8 5.9 reshape.55
  40.7 0.1 copy.21
  40.8 54.5 %while.11 = (s32[]{:T(128)}, bf16[2,16,64,512]{3,2,1,0:T(8,128)(2,1)}, bf16[2,16,64,512]{3,2,1,0:T(8,128)(2,1)}, s32[2,16,8]{2,1,0:T(8,128)S(1)}, bf16[48,32768]{1,0:T(8,128)(2,1)}, /*index=5*/s32[]{:T(128)}) while((s32[]{:T(128)}, bf16[2,16,64,512]{3,2,1,0:T(8,128)(2,1)}, bf16[2,16,64,512]{3,2,1,0:T(8,128)(2,1)}, ...), condition=%wide.region_3.4_spmd.clone, body=%wide.region_2.3_spmd.clone.sunk | while | flops 944248832 | bytes 38800968 | solution.py:44
  40.8 0.1 eq.105
  40.9 7.5 %convolution_convert_fusion.4 = bf16[128,32768]{1,0:T(8,128)(2,1)} fusion(bf16[48,32768]{1,0:T(8,128)(2,1)} %get-tuple-element.109, s32[128]{0:T(128)S(1)} %eq.105), kind=kOutput, calls=%fused_computation.1.clone.1 | convolution fusion | flops 406853632 | bytes 11534848 | tf_op jit(solution)/shard_map/while/body/eval_jaxpr/dot_general | solution.py:32
  48.4 13.5 %reshape.70 = bf16[16,512,512]{2,1,0:T(8,128)(2,1)} reshape(bf16[128,32768]{1,0:T(8,128)(2,1)} %convolution_convert_fusion.4) | data formatting | bytes 16777216 | tf_op jit(solution)/shard_map/while/body/eval_jaxpr/reshape | solution.py:35
  61.9 6.1 %fusion.27 = bf16[2,16,64,512]{3,2,1,0:T(8,128)(2,1)} fusion(bf16[2,16,64,512]{3,2,1,0:T(8,128)(2,1)} %get-tuple-element.100, s32[]{:T(128)} %get-tuple-element.99, bf16[16,512,512]{2,1,0:T(8,128)(2,1)} %reshape.70, bf16[2,16,64,512]{3,2,1,0:T(8,128)(2,1)} %get-tuple-element.107), kind=kOutput, calls=%fused_computation.4.clone.1 | convolution fusion | flops 537395200 | bytes 10486784 | tf_op jit(solution)/shard_map/while/body/eval_jaxpr/pim,pmc->pic/dot_general | solution.py:36
  68.0 0.1 eq.105
  68.1 7.5 %convolution_convert_fusion.4 = bf16[128,32768]{1,0:T(8,128)(2,1)} fusion(bf16[48,32768]{1,0:T(8,128)(2,1)} %get-tuple-element.109, s32[128]{0:T(128)S(1)} %eq.105), kind=kOutput, calls=%fused_computation.1.clone.1 | convolution fusion | flops 406853632 | bytes 11534848 | tf_op jit(solution)/shard_map/while/body/eval_jaxpr/dot_general | solution.py:32
  75.6 13.5 %reshape.70 = bf16[16,512,512]{2,1,0:T(8,128)(2,1)} reshape(bf16[128,32768]{1,0:T(8,128)(2,1)} %convolution_convert_fusion.4) | data formatting | bytes 16777216 | tf_op jit(solution)/shard_map/while/body/eval_jaxpr/reshape | solution.py:35
  89.1 6.2 %fusion.27 = bf16[2,16,64,512]{3,2,1,0:T(8,128)(2,1)} fusion(bf16[2,16,64,512]{3,2,1,0:T(8,128)(2,1)} %get-tuple-element.100, s32[]{:T(128)} %get-tuple-element.99, bf16[16,512,512]{2,1,0:T(8,128)(2,1)} %reshape.70, bf16[2,16,64,512]{3,2,1,0:T(8,128)(2,1)} %get-tuple-element.107), kind=kOutput, calls=%fused_computation.4.clone.1 | convolution fusion | flops 537395200 | bytes 10486784 | tf_op jit(solution)/shard_map/while/body/eval_jaxpr/pim,pmc->pic/dot_general | solution.py:36
  95.3 2.8 copy.25
  98.0 8.2 %convolution_convert_fusion.2 = bf16[256,32768]{1,0:T(8,128)(2,1)} fusion(bf16[32,32768]{1,0:T(8,128)(2,1)S(1)} %bitcast.39, s32[32]{0:T(128)S(1)} %get-tuple-element.60), kind=kOutput, calls=%fused_computation.11 | convolution fusion | flops 545267712 | bytes 18874496 | tf_op jit(solution)/shard_map/dot_general | solution.py:54
  106.2 27.0 %all_to_all.13 = bf16[128,2,32768]{2,1,0:T(2,128)(2,1)} reshape(bf16[256,32768]{1,0:T(8,128)(2,1)} %convolution_convert_fusion.2) | data formatting | bytes 33554432 | tf_op jit(solution)/shard_map/all_to_all | solution.py:60
  133.2 14.0 %all-to-all-start.1 = ((bf16[128,2,32768]{2,1,0:T(2,128)(2,1)}), bf16[128,2,32768]{2,1,0:T(2,128)(2,1)}, u32[]{:S(2)}, u32[]{:S(2)}) async-start(bf16[128,2,32768]{2,1,0:T(2,128)(2,1)} %all_to_all.13), calls=%async_computation.1 | async-start | bytes 33554432 | tf_op jit(solution)/shard_map/all_to_all | solution.py:60
  147.3 0.5 broadcast.26
  147.8 0.8 reduce.3
  148.6 0.1 eq.62
  148.7 376.1 %all-to-all-done.1 = bf16[128,2,32768]{2,1,0:T(2,128)(2,1)} async-done(((bf16[128,2,32768]{2,1,0:T(2,128)(2,1)}), bf16[128,2,32768]{2,1,0:T(2,128)(2,1)}, u32[]{:S(2)}, u32[]{:S(2)}) %all-to-all-start.1) | async-done | bytes 16777248 | tf_op jit(solution)/shard_map/all_to_all | solution.py:60
  524.8 25.0 %all_to_all.15 = bf16[256,32768]{1,0:T(8,128)(2,1)} reshape(bf16[128,2,32768]{2,1,0:T(2,128)(2,1)} %all-to-all-done.1) | data formatting | bytes 33554432 | tf_op jit(solution)/shard_map/all_to_all | solution.py:60
  549.8 10.6 %fusion.10 = f32[32,32768]{1,0:T(8,128)} fusion(bf16[256,32768]{1,0:T(8,128)(2,1)} %all_to_all.15, s32[256]{0:T(256)S(1)} %eq.62), kind=kOutput, calls=%fused_computation.20 | convolution fusion | flops 536879104 | bytes 20972544 | tf_op jit(solution)/shard_map/dot_general | solution.py:64
  560.4 4.9 reshape.57
  565.3 4.0 divide_convert_fusion
  569.3 16.5 %all-gather.2.cloned.1.call-done = bf16[2048,1024]{1,0:T(8,128)(2,1)} async-done(((bf16[2048,512]{1,0:T(8,128)(2,1)}), bf16[2048,1024]{1,0:T(8,128)(2,1)}) %all-gather.2.cloned.1.call-update) | async-done | bytes 4194320 | tf_op jit(solution)/shard_map/all_gather | solution.py:68
  585.8 6.0 maximum_convert_fusion
  (23 shorter events, 0.1 us)
Async XLA Ops:
  6.5 18.9 %copy-start = (bf16[3,1,512,512]{3,2,1,0:T(8,128)(2,1)S(1)}, bf16[3,1,512,512]{3,2,1,0:T(8,128)(2,1)}, u32[]{:S(2)}) copy-start(bf16[3,1,512,512]{3,2,1,0:T(8,128)(2,1)} %param.13) | copy-start | bytes 4718596
  9.0 124.1 %all-to-all-start = ((s32[128,2,1]{1,2,0:T(1,128)}), s32[128,2,1]{1,2,0:T(1,128)S(1)}, u32[]{:S(2)}, u32[]{:S(2)}) async-start(s32[128,2,1]{1,2,0:T(1,128)} %bitcast.1), calls=%async_computation | async-start | bytes 131072 | tf_op jit(solution)/shard_map/all_to_all | solution.py:61
  34.8 5.9 copy-start.3
  34.8 5.9 copy-start.4
  133.2 14.1 %copy-start.2 = (s32[2048]{0:T(1024)S(1)}, s32[2048]{0:T(1024)}, u32[]{:S(2)}) copy-start(s32[2048]{0:T(1024)} %param.19) | copy-start | bytes 24580
  133.2 391.7 %all-to-all-start.1 = ((bf16[128,2,32768]{2,1,0:T(2,128)(2,1)}), bf16[128,2,32768]{2,1,0:T(2,128)(2,1)}, u32[]{:S(2)}, u32[]{:S(2)}) async-start(bf16[128,2,32768]{2,1,0:T(2,128)(2,1)} %all_to_all.13), calls=%async_computation.1 | async-start | bytes 33554432 | tf_op jit(solution)/shard_map/all_to_all | solution.py:60
  147.2 438.6 %all-gather.2.cloned.1.call-start = ((), (), s32[]{:S(2)}) async-start(), calls=%async_computation.2 | async-start | bytes 6291456 | tf_op jit(solution)/shard_map/all_gather | solution.py:68
  565.3 20.5 %copy-start.5 = (bf16[1024,512]{1,0:T(8,128)(2,1)S(1)}, bf16[1024,512]{1,0:T(8,128)(2,1)}, u32[]{:S(2)}) copy-start(bf16[1024,512]{1,0:T(8,128)(2,1)} %param.20) | copy-start | bytes 3145732
  565.3 20.5 %copy-start.6 = (f32[512]{0:T(512)S(1)}, f32[512]{0:T(512)}, u32[]{:S(2)}) copy-start(f32[512]{0:T(512)} %param.21) | copy-start | bytes 6148
  585.8 6.0 copy-start.1
Sparse Core Ops, SparseCore 0:
  569.4 16.2 all-gather.1
where the time goes:
time: 601 us; the launch traced here: 599 us
  waiting for transfers between devices  393 us (65%)
  local copies, waits for them, and re-layouts  98.9 us (16%)
  matrix products  56.8 us (9%)
  starting transfers between devices  30.4 us (5%)
  between operations  13.5 us (2%)
  other arithmetic  6.52 us (1%)
    all_to_all x1, waiting for transfers between devices, local(): lax.all_to_all(outgoing, 'rows', split_axis=0, concat_axis=0, tiled=True)  376 us
    all_to_all x2, local copies, waits for them, and re-layouts, local(): lax.all_to_all(outgoing, 'rows', split_axis=0, concat_axis=0, tiled=True)  52 us
    reshape x2, local copies, waits for them, and re-layouts, partial_group(): picked = picked.reshape(per_turn, per_row * tile, half_w)  26.9 us
    all_gather x1, waiting for transfers between devices, local(): lax.all_gather(agg, 'half', axis=1, tiled=True)  16.5 us
    all_to_all x1, starting transfers between devices, local(): lax.all_to_all(out_ids, 'rows', split_axis=0, concat_axis=0, tiled=True)  16.3 us
    dot_general x2, matrix products, partial_group(): jnp.dot(chooser, flat_blocks, preferred_element_type=jnp.float32)  15 us
    all_to_all x1, starting transfers between devices, local(): lax.all_to_all(outgoing, 'rows', split_axis=0, concat_axis=0, tiled=True)  14 us
    dot_general x2, matrix products, partial_group(): jnp.einsum('pim,pmc->pic', group_tiles, picked, preferred_element_type=jn...  12.3 us
  transfers between devices with their start and end apart: 3, of which 2 were waited for; matrix products, arithmetic and copies ran while one was open for 14% of the time, Pallas kernels for 0%

commit v1 on v0

v1 whole, which is shorter than its diff:
```python
import functools

import jax
import jax.numpy as jnp
from jax import lax
from jax.experimental import pallas as pl
from jax.experimental.pallas import tpu as pltpu
from jax.sharding import PartitionSpec as P

MESH = pl.DeviceIdType.MESH
NZ, NX, NY = 8, 4, 4
ROWS = NZ * NX * NY
TILE = 64
LB = 32

Z_LOCAL, Z_CAP = 12, (24, 20, 14, 6)
X_LOCAL, X_CAP = 40, (40, 20)
MERGE = 144
Y_FAR = LB // 2
Y_LIST = LB + Y_FAR

COLS = 128
HEIGHT = 32
COL_CHUNKS = 4
ROW_CHUNKS = TILE // HEIGHT
CHUNKS = COL_CHUNKS * ROW_CHUNKS


def bases(local, caps, start):
    right, left, at = [], [], start + local
    for cap in caps:
        right.append(at)
        at += cap
    for cap in caps:
        left.append(at)
        at += cap
    return right, left, at


Z_RIGHT, Z_LEFT, Z_SLOTS = bases(Z_LOCAL, Z_CAP, 0)
X_RIGHT, X_LEFT, X_SLOTS = bases(X_LOCAL, X_CAP, 1)


def tri(n):
    return (jnp.arange(n)[:, None] < jnp.arange(n)[None, :]).astype(jnp.bfloat16)


def before(masks):
    shape = masks.shape
    flat = masks.astype(jnp.bfloat16).reshape(-1, shape[-1])
    counts = jnp.dot(flat, tri(shape[-1]), preferred_element_type=jnp.float32)
    return counts.astype(jnp.int32).reshape(shape)


def listed(delta, ring, n_caps, right_base, left_base, local_base):
    half = ring // 2
    tie = delta == half
    odd = before(tie) % 2
    to_right = ((delta >= 1) & (delta < half)) | (tie & (odd == 0))
    to_left = ((delta > half) & (delta < ring)) | (tie & (odd == 1))
    dist = jnp.where(delta <= half, delta, ring - delta)
    masks = [delta == 0]
    masks += [to_right & (dist == k) for k in range(1, half + 1)]
    masks += [to_left & (dist == k) for k in range(1, half + 1)]
    masks = jnp.stack(masks)
    ranks = before(masks)
    totals = jnp.sum(masks.astype(jnp.int32), axis=-1, keepdims=True)
    place = jnp.where(masks[0], ranks[0], 0)
    address = jnp.where(masks[0], local_base + ranks[0], 0)
    for side, base in ((0, right_base), (1, left_base)):
        farther = jnp.zeros_like(totals[0])
        for k in range(half, 0, -1):
            at = 1 + side * half + k - 1
            spot = farther + ranks[at]
            place = jnp.where(masks[at], spot, place)
            address = jnp.where(masks[at], base[k - 1] + spot, address)
            farther = farther + totals[at]
    which = jnp.where(to_right, 1, 0) + jnp.where(to_left, 2, 0)
    return address, which, place


def table(value, valid, which, place, sizes):
    parts = []
    for number, size in enumerate(sizes):
        spot = jnp.arange(size)[:, None]
        hit = (place[None, :] == spot) & ((which == number) & valid)[None, :]
        parts.append(jnp.sum(jnp.where(hit, value[None, :], 0), axis=1))
    return jnp.concatenate(parts).astype(jnp.int32)


def tables(keys, me):
    owner, block = keys // LB, keys % LB
    dz, dx, dy = owner // (NX * NY), (owner // NY) % NX, owner % NY
    number = jnp.arange(ROWS)
    sz, sx, sy = number // (NX * NY), (number // NY) % NX, number % NY
    mz, mx, my = me // (NX * NY), (me // NY) % NX, me % NY

    grid = lambda a: lax.dynamic_index_in_dim(a.reshape(NZ, NX, NY, -1), my, 2, keepdims=False)
    gz, gx, gy, gb = grid(dz), grid(dx), grid(dy), grid(block)
    z_delta = (gz - jnp.arange(NZ)[:, None, None]) % NZ
    z_addr, z_which, z_place = listed(z_delta, NZ, len(Z_CAP), Z_RIGHT, Z_LEFT, 0)
    mine = lambda a: lax.dynamic_index_in_dim(
        lax.dynamic_index_in_dim(a, mz, 0, keepdims=False), mx, 0, keepdims=False
    )
    parts = keys.shape[1]
    z_tab = table(
        jnp.arange(parts), jnp.ones((parts,), bool), mine(z_which), mine(z_place),
        (Z_LOCAL, Z_CAP[0], Z_CAP[0]),
    )

    lines = lambda a: a.transpose(1, 0, 2).reshape(NX, NZ * parts)
    here = lines(gz) == mz
    lx = lines(gx)
    x_delta = jnp.where(here, (lx - jnp.arange(NX)[:, None]) % NX, NX)
    x_addr, x_which, x_place = listed(x_delta, NX, len(X_CAP), X_RIGHT, X_LEFT, 1)
    line = lambda a: lax.dynamic_index_in_dim(a, mx, 0, keepdims=False)
    x_tab = table(
        line(lines(z_addr)), line(here), line(x_which), line(x_place),
        (X_LOCAL, X_CAP[0], X_CAP[0]),
    )

    arrived = (here & (lx == mx)).reshape(-1)
    y_delta = (lines(gy).reshape(-1) - my) % NY
    lb = lines(gb).reshape(-1)
    target = jnp.where(
        y_delta == 0,
        lb,
        jnp.where(
            y_delta == 1,
            LB + Y_FAR + lb,
            jnp.where(
                y_delta == 3,
                LB + Y_LIST + Y_FAR + lb,
                jnp.where(lb < Y_FAR, LB + lb, LB + Y_LIST + lb - Y_FAR),
            ),
        ),
    )
    n_targets = LB + 2 * Y_LIST
    onehot = (target[None, :] == jnp.arange(n_targets)[:, None]) & arrived[None, :]
    hist = jnp.sum(onehot.astype(jnp.int32), axis=1)
    earlier = jnp.arange(n_targets)[None, :] < jnp.arange(n_targets)[:, None]
    start = jnp.sum(jnp.where(earlier, hist[None, :], 0), axis=1)
    rank = before(onehot)
    spot = jnp.sum(jnp.where(onehot, rank + start[:, None], 0), axis=0)
    seat = jnp.arange(MERGE)[:, None]
    address = x_addr.reshape(-1)
    y_src = jnp.sum(
        jnp.where((spot[None, :] == seat) & arrived[None, :], address[None, :], 0), axis=1
    )
    y_first = jnp.sum(
        ((start[None, :] == seat) & (hist > 0)[None, :]).astype(jnp.int32), axis=1
    )
    y_last = jnp.where(hist > 0, start + hist - 1, MERGE)

    def ring_fits(counts, local, caps):
        ring = counts.shape[0]
        half = ring // 2
        tied = counts[half]
        ok = jnp.all(counts[0] <= local)
        for side in (0, 1):
            far = (tied + 1 - side) // 2
            ok &= jnp.all(far <= caps[half - 1])
            for k in range(half - 1, 0, -1):
                far = far + counts[k if side == 0 else ring - k]
                ok &= jnp.all(far <= caps[k - 1])
        return ok

    all_z = (dz - sz[:, None]) % NZ
    z_counts = jnp.stack([jnp.sum((all_z == k).astype(jnp.int32), axis=1) for k in range(NZ)])
    fits = ring_fits(z_counts, Z_LOCAL, Z_CAP)
    holder = (dz * NX * NY + (sx * NY + sy)[:, None]).reshape(1, -1)
    holds = (holder == number[:, None]).astype(jnp.bfloat16)
    goes = (((dx - sx[:, None]) % NX).reshape(1, -1) == jnp.arange(NX)[:, None]).astype(jnp.bfloat16)
    x_counts = lax.dot_general(
        goes, holds, (((1,), (1,)), ((), ())), preferred_element_type=jnp.float32
    ).astype(jnp.int32)
    fits &= ring_fits(x_counts, X_LOCAL, X_CAP)
    by_x = x_counts.reshape(NX, NZ, NX, NY)
    for dest in range(NX):
        total = sum(by_x[(dest - at) % NX, :, at, :] for at in range(NX))
        fits &= jnp.all(total <= MERGE)
    y_tab = jnp.concatenate([y_src, y_first, y_last]).astype(jnp.int32)
    return z_tab, x_tab, y_tab, fits


def partials_kernel(picks, feats, weight, tiles, out, msgs):
    n_rel, per = weight.shape[0], feats.shape[0] // TILE
    step = 256
    for r in range(n_rel):
        for s in range(feats.shape[0] // step):
            m = jnp.dot(
                feats[s * step : (s + 1) * step, :], weight[r], preferred_element_type=jnp.float32
            ).astype(jnp.bfloat16)
            at = r * per + s * (step // TILE)
            msgs[at : at + step // TILE] = m.reshape(step // TILE, TILE, m.shape[1])
    kt = tiles.shape[2] // TILE

    def one(p, carry):
        rhs = jnp.concatenate([msgs[picks[p * kt + k]] for k in range(kt)], axis=0)
        v = jnp.dot(tiles[p], rhs, preferred_element_type=jnp.float32).astype(jnp.bfloat16)
        for i in range(ROW_CHUNKS):
            for j in range(COL_CHUNKS):
                out[i * COL_CHUNKS + j, p] = v[
                    i * HEIGHT : (i + 1) * HEIGHT, j * COLS : (j + 1) * COLS
                ]
        return carry

    lax.fori_loop(0, tiles.shape[0], one, 0)


def schedule():
    unit = 1.41 * 2 / CHUNKS / 2
    rings = {
        "z": [c * unit for c in Z_CAP],
        "x": [c * unit for c in X_CAP],
        "y": [Y_LIST * unit, Y_FAR * unit],
    }
    work = {"z": 1.0, "x": 1.0, "y": 3.5, "f": 1.5, "g": 1.5}
    free = {"z": 0.0, "x": 0.0, "y": 0.0, "h": 0.0}
    now, order = 0.0, []
    ready = {("z", 0, c): 0.0 for c in range(CHUNKS)}
    while ready:
        best = None
        for (kind, k, c), t in ready.items():
            start = max(t, now)
            if kind == "z" and k == 0:
                start = max(start, free["z"] - 2.5)
            rank = (start, 0 if k > 0 else 1, c)
            if best is None or rank < best[0]:
                best = (rank, (kind, k, c), start)
        _, (kind, k, c), start = best
        del ready[(kind, k, c)]
        order.append((kind, k, c))
        now = start + (work[kind] if k == 0 else 0.1)
        if kind in rings:
            sends = rings[kind]
            if k < len(sends):
                free[kind] = max(free[kind], now) + sends[k]
                ready[(kind, k + 1, c)] = free[kind] + 1.8
            if k == len(sends):
                follow = {"z": "x", "x": "y", "y": "f"}[kind]
                ready[(follow, 0, c)] = now
        elif kind == "f":
            free["h"] = max(free["h"], now) + 0.8
            ready[("g", 0, c)] = free["h"] + 1.0
    return order


def route_kernel(order, *refs):
    it = iter(refs)
    z_tab, x_tab, y_tab, part, degree, mix, bias, out = [next(it) for _ in range(8)]
    zs = [next(it) for _ in range(CHUNKS)]
    zb = [next(it) for _ in range(CHUNKS)]
    xs = [next(it) for _ in range(CHUNKS)]
    xb = [next(it) for _ in range(CHUNKS)]
    ys = [next(it) for _ in range(CHUNKS)]
    yr = [next(it) for _ in range(CHUNKS)]
    ag = [next(it) for _ in range(CHUNKS)]
    stage, total = next(it), next(it)
    z_send, z_recv, x_send, x_recv, y_send, y_recv, h_send, h_recv = [next(it) for _ in range(8)]

    me, half = lax.axis_index("rows"), lax.axis_index("half")
    mz, mx, my = me // (NX * NY), (me // NY) % NX, me % NY

    def at(z, x, y):
        return {"rows": (z % NZ) * (NX * NY) + (x % NX) * NY + y % NY}

    zp, zm = at(mz + 1, mx, my), at(mz + NZ - 1, mx, my)
    xp, xm = at(mz, mx + 1, my), at(mz, mx + NX - 1, my)
    yp, ym = at(mz, mx, my + 1), at(mz, mx, my + NY - 1)
    other = {"half": 1 - half}

    barrier = pltpu.get_barrier_semaphore()
    neighbours = (zp, zm, xp, xm, yp, ym, other)
    for device in neighbours:
        pl.semaphore_signal(barrier, inc=1, device_id=device, device_id_type=MESH)
    pl.semaphore_wait(barrier, len(neighbours))

    def gather(dst, base, read, tab, off, n):
        def body(j, carry):
            dst[base + j] = read(tab[off + j])
            return carry

        lax.fori_loop(0, n, body, 0, unroll=4)

    def copy(src, dst, send, recv, device):
        return pltpu.make_async_remote_copy(
            src_ref=src, dst_ref=dst, send_sem=send, recv_sem=recv,
            device_id=device, device_id_type=MESH,
        )

    def z_copies(c, k):
        n = Z_CAP[k]
        result = []
        for side, device, base in ((0, zp, Z_RIGHT), (1, zm, Z_LEFT)):
            if k == 0:
                src = zs[c].at[pl.ds(side * n, n)]
            else:
                src = zb[c].at[pl.ds(base[k - 1], n)]
            dst = zb[c].at[pl.ds(base[k], n)]
            result.append(copy(src, dst, z_send.at[c, k, side], z_recv.at[c, k, side], device))
        return result

    def x_copies(c, k):
        n = X_CAP[k]
        result = []
        for side, device, base in ((0, xp, X_RIGHT), (1, xm, X_LEFT)):
            if k == 0:
                src = xs[c].at[pl.ds(side * n, n)]
            else:
                src = xb[c].at[pl.ds(base[k - 1], n)]
            dst = xb[c].at[pl.ds(base[k], n)]
            result.append(copy(src, dst, x_send.at[c, k, side], x_recv.at[c, k, side], device))
        return result

    def y_copies(c, k):
        result = []
        for side, device in ((0, yp), (1, ym)):
            if k == 0:
                src = ys[c].at[pl.ds(LB + side * Y_LIST, Y_LIST)]
                dst = yr[c].at[pl.ds(side * Y_LIST, Y_LIST)]
            else:
                src = yr[c].at[pl.ds(side * Y_LIST, Y_FAR)]
                dst = yr[c].at[pl.ds(2 * Y_LIST + side * Y_FAR, Y_FAR)]
            result.append(copy(src, dst, y_send.at[c, k, side], y_recv.at[c, k, side], device))
        return result

    def h_copy(c):
        return copy(ag[c].at[half], ag[c].at[half], h_send.at[c], h_recv.at[c], other)

    stage[MERGE] = jnp.zeros(stage.shape[1:], stage.dtype)
    for c in range(CHUNKS):
        xb[c][0] = jnp.zeros(xb[c].shape[1:], xb[c].dtype)

    ring = {"z": (z_copies, len(Z_CAP)), "x": (x_copies, len(X_CAP)), "y": (y_copies, 2)}

    for kind, k, c in order:
        row, col = c // COL_CHUNKS, c % COL_CHUNKS
        if kind in ring and k > 0:
            copies, hops = ring[kind]
            for item in copies(c, k - 1):
                item.wait_recv()
            if k < hops:
                for item in copies(c, k):
                    item.start()
        elif kind == "z":
            read = lambda i: part[c, i]
            gather(zs[c], 0, read, z_tab, Z_LOCAL, 2 * Z_CAP[0])
            for item in z_copies(c, 0):
                item.start()
            gather(zb[c], 0, read, z_tab, 0, Z_LOCAL)
        elif kind == "x":
            read = lambda i: zb[c][i]
            gather(xs[c], 0, read, x_tab, X_LOCAL, 2 * X_CAP[0])
            for item in x_copies(c, 0):
                item.start()
            gather(xb[c], 1, read, x_tab, 0, X_LOCAL)
        elif kind == "y":

            def add(j, total_now):
                v = xb[c][y_tab[j]].astype(jnp.float32)
                total_now = jnp.where(y_tab[MERGE + j] > 0, v, total_now + v)
                stage[j] = total_now.astype(stage.dtype)
                return total_now

            lax.fori_loop(0, MERGE, add, jnp.zeros((HEIGHT, COLS), jnp.float32), unroll=4)
            read = lambda i: stage[i]
            gather(ys[c], LB, read, y_tab, 2 * MERGE + LB, 2 * Y_LIST)
            for item in y_copies(c, 0):
                item.start()
            gather(ys[c], 0, read, y_tab, 2 * MERGE, LB)
        elif kind == "f":

            def finish(b, carry):
                v = ys[c][b].astype(jnp.float32) + yr[c][Y_FAR + b].astype(jnp.float32)
                v = v + yr[c][Y_LIST + Y_FAR + b].astype(jnp.float32)
                v = v + yr[c][2 * Y_LIST + b].astype(jnp.float32)
                v = v / degree[b, row * HEIGHT : (row + 1) * HEIGHT, :]
                ag[c][half, b] = v.astype(jnp.bfloat16)
                return carry

            lax.fori_loop(0, LB, finish, 0, unroll=2)
            h_copy(c).start()
        else:
            h_copy(c).wait_recv()
            some = 8
            width = mix.shape[0] // 2
            w = jnp.concatenate(
                [
                    mix[col * COLS : (col + 1) * COLS, :],
                    mix[width + col * COLS : width + (col + 1) * COLS, :],
                ],
                axis=0,
            )

            def mixing(b, carry):
                blocks = pl.ds(b * some, some)
                a = jnp.concatenate(
                    [
                        ag[c][0, blocks].reshape(some * HEIGHT, COLS),
                        ag[c][1, blocks].reshape(some * HEIGHT, COLS),
                    ],
                    axis=1,
                )
                v = jnp.dot(a, w, preferred_element_type=jnp.float32)
                v = v.reshape(some, HEIGHT, v.shape[1])
                if col > 0:
                    v = v + total[blocks]
                if col < COL_CHUNKS - 1:
                    total[blocks] = v
                else:
                    v = jnp.maximum(v + bias[...][None], 0.0)
                    out[blocks, row * HEIGHT : (row + 1) * HEIGHT, :] = v.astype(out.dtype)
                return carry

            lax.fori_loop(0, LB // some, mixing, 0)

    for c in range(CHUNKS):
        for copies, hops in ring.values():
            for k in range(hops):
                for item in copies(c, k):
                    item.wait_send()
        h_copy(c).wait_send()


def vmem():
    return pl.BlockSpec(memory_space=pltpu.VMEM)


def smem():
    return pl.BlockSpec(memory_space=pltpu.SMEM)


def local(
    source_feats, rel_weight, tiles, src_blk, rel_id, owner, local_blk, in_degree, mix_weight, bias
):
    n_rows = lax.axis_size("rows")
    src_dev, half_w = source_feats.shape
    tile = tiles.shape[1]
    parts, per_row = src_blk.shape
    n_rel = rel_weight.shape[0]
    n_src_blocks = src_dev // tile
    n_local = in_degree.shape[0] // tile

    keys = lax.all_gather(owner[:, 0] * LB + local_blk, "rows", axis=0, tiled=False)
    picks = (rel_id * n_src_blocks + src_blk).reshape(-1)
    part = pl.pallas_call(
        partials_kernel,
        out_shape=jax.ShapeDtypeStruct((CHUNKS, parts, HEIGHT, COLS), jnp.bfloat16),
        in_specs=[smem(), vmem(), vmem(), vmem()],
        out_specs=vmem(),
        scratch_shapes=[pltpu.VMEM((n_rel * n_src_blocks, tile, half_w), jnp.bfloat16)],
        cost_estimate=pl.CostEstimate(
            flops=2 * half_w * half_w * (src_dev * n_rel + parts * tile),
            bytes_accessed=7 << 20,
            transcendentals=0,
        ),
    )(picks, source_feats, rel_weight[:, 0], tiles)
    z_tab, x_tab, y_tab, fits = tables(keys, lax.axis_index("rows"))
    degree = in_degree.astype(jnp.float32)

    def routed(part):
        wide = jnp.broadcast_to(degree[:, None], (degree.shape[0], COLS)).reshape(n_local, tile, COLS)
        block = lambda n: [pltpu.VMEM((n, HEIGHT, COLS), jnp.bfloat16)] * CHUNKS
        dma = pltpu.SemaphoreType.DMA
        out = pl.pallas_call(
            functools.partial(route_kernel, schedule()),
            out_shape=jax.ShapeDtypeStruct((n_local, tile, half_w), jnp.bfloat16),
            in_specs=[smem(), smem(), smem()] + [vmem()] * 4,
            out_specs=vmem(),
            scratch_shapes=block(2 * Z_CAP[0])
            + block(Z_SLOTS)
            + block(2 * X_CAP[0])
            + block(X_SLOTS)
            + block(LB + 2 * Y_LIST)
            + block(2 * Y_LIST + 2 * Y_FAR)
            + [pltpu.VMEM((2, n_local, HEIGHT, COLS), jnp.bfloat16)] * CHUNKS
            + [
                pltpu.VMEM((MERGE + 1, HEIGHT, COLS), jnp.bfloat16),
                pltpu.VMEM((n_local, HEIGHT, half_w), jnp.float32),
                dma((CHUNKS, len(Z_CAP), 2)),
                dma((CHUNKS, len(Z_CAP), 2)),
                dma((CHUNKS, len(X_CAP), 2)),
                dma((CHUNKS, len(X_CAP), 2)),
                dma((CHUNKS, 2, 2)),
                dma((CHUNKS, 2, 2)),
                dma((CHUNKS,)),
                dma((CHUNKS,)),
            ],
            compiler_params=pltpu.CompilerParams(
                collective_id=0, has_side_effects=True, vmem_limit_bytes=64 * 1024 * 1000
            ),
        )(z_tab, x_tab, y_tab, part, wide, mix_weight, bias[None, :])
        return out.reshape(n_local * tile, half_w)

    def dense(part):
        capacity = max(2, 2 * parts // n_rows)
        partials = part.reshape(ROW_CHUNKS, COL_CHUNKS, parts, HEIGHT, COLS)
        partials = partials.transpose(2, 0, 3, 1, 4).reshape(parts, tile * half_w)
        target_dev = owner[:, 0]
        positions = jnp.arange(parts, dtype=jnp.int32)
        earlier = (target_dev[:, None] == target_dev[None, :]) & (
            positions[None, :] < positions[:, None]
        )
        rank = jnp.sum(earlier.astype(jnp.int32), axis=1)
        slot = target_dev * capacity + rank
        slot_ids = jnp.arange(n_rows * capacity, dtype=jnp.int32)
        placing = slot_ids[:, None] == slot[None, :]
        outgoing = jnp.dot(
            placing.astype(jnp.bfloat16), partials, preferred_element_type=jnp.float32
        ).astype(jnp.bfloat16)
        out_ids = jnp.sum(jnp.where(placing, local_blk[None, :] + 1, 0), axis=1) - 1
        block_index = jnp.arange(n_local, dtype=jnp.int32)
        arrived = lax.all_to_all(outgoing, "rows", split_axis=0, concat_axis=0, tiled=True)
        arrived_ids = lax.all_to_all(out_ids, "rows", split_axis=0, concat_axis=0, tiled=True)
        selector = (arrived_ids[None, :] == block_index[:, None]).astype(jnp.bfloat16)
        summed = jnp.dot(selector, arrived, preferred_element_type=jnp.float32)
        summed = summed.reshape(n_local * tile, half_w)
        agg = (summed / degree[:, None]).astype(jnp.bfloat16)
        theirs = lax.ppermute(agg, "half", [(0, 1), (1, 0)])
        half = lax.axis_index("half")
        w_mine = lax.dynamic_slice_in_dim(mix_weight, half * half_w, half_w, 0)
        w_theirs = lax.dynamic_slice_in_dim(mix_weight, (1 - half) * half_w, half_w, 0)
        mixed = jnp.dot(
            jnp.concatenate([agg, theirs], axis=1),
            jnp.concatenate([w_mine, w_theirs], axis=0),
            preferred_element_type=jnp.float32,
        )
        return jax.nn.relu(mixed + bias).astype(jnp.bfloat16)

    return lax.cond(fits, routed, dense, part)


def solution(mesh):
    placed = (
        P("rows", "half"),
        P(None, "half", None, None),
        P("rows", None, None),
        P("rows", None),
        P("rows", None),
        P("rows", None),
        P("rows"),
        P("rows"),
        P(None, "half"),
        P("half"),
    )
    return jax.shard_map(
        local, mesh=mesh, in_specs=placed, out_specs=P("rows", "half"), check_vma=False
    )
```

time: 601 us -> 906 us (1.51)
  blocking collectives: 0 us -> 583 us
  waiting for transfers between devices: 393 us -> 0 us
  Pallas kernels: 0 us -> 288 us
  local copies, waits for them, and re-layouts: 98.9 us -> 9.41 us
  matrix products: 56.8 us -> 1.65 us
  starting transfers between devices: 30.4 us -> 0 us
    unnamed x0 -> x1, blocking collectives: none -> 583 us
    all_to_all x2 -> x0, waiting for transfers between devices: 376 us -> none  [the longest x1 376 us: local(): lax.all_to_all(outgoing, 'rows', split_axis=0, concat_axis=0, tiled=True)]
    pallas_call x0 -> x2, Pallas kernels: none -> 288 us  [the longest x1 276 us: routed(): pl.pallas_call(functools.partial(route_kernel, schedule()), out_shape=jax...]
    dot_general x8 -> x6, matrix products: 56.8 us -> 1.65 us  [the longest x5 1.21 us: before(): counts = jnp.dot(flat, tri(shape[-1]), preferred_element_type=jnp.float32)]
    all_to_all x3 -> x0, local copies, waits for them, and re-layouts: 52.5 us -> none  [the longest x2 52 us: local(): lax.all_to_all(outgoing, 'rows', split_axis=0, concat_axis=0, tiled=True)]
    reshape x4 -> x6, local copies, waits for them, and re-layouts: 37.8 us -> 1.07 us  [the longest x1 0.68 us: local(): picks = (rel_id * n_src_blocks + src_blk).reshape(-1)]
    all_to_all x2 -> x0, starting transfers between devices: 30.4 us -> none  [the longest x1 16.3 us: local(): lax.all_to_all(out_ids, 'rows', split_axis=0, concat_axis=0, tiled=True)]
    all_gather x1 -> x0, waiting for transfers between devices: 16.5 us -> none  [local(): lax.all_gather(agg, 'half', axis=1, tiled=True)]
  transfers between devices with their start and end apart: 3 -> 0, of which waited for: 2 -> 0; matrix products, arithmetic and copies ran while one was open for 14% -> 0% of each run, Pallas kernels for 0% -> 0%
where the time goes in v1:
time: 906 us; the launch traced here: 905 us
  blocking collectives  583 us (64%)
  Pallas kernels  288 us (32%)
  between operations  12.5 us (1%)
  other arithmetic  9.8 us (1%)
  local copies, waits for them, and re-layouts  9.41 us (1%)
    unnamed x1, blocking collectives  583 us
    pallas_call x1, Pallas kernels, routed(): pl.pallas_call(functools.partial(route_kernel, schedule()), out_shape=jax...  276 us

profile of v1, /device:TPU:1, one launch (start us, length us, event | category | flops | bytes accessed | tf_op | source)
XLA Modules:
  0.0 905.0 jit_solution(15265367517876934850)
XLA Ops:
  0.0 1.3 dynamic-slice.4
  1.9 0.8 fusion.88
  2.7 583.1 %all-reduce = s32[4096]{0:T(1024)S(1)} all-reduce(s32[4096]{0:T(1024)S(1)} %fusion.88), channel_id=2, replica_groups=mesh['rows'=128,'half'=2] {'rows'}, use_global_device_ids=true, to_apply=%add | all-reduce | flops 4096 | bytes 32768
  585.9 0.2 add_select_fusion.2
  586.1 0.3 convert_reduce_fusion.4
  586.4 0.6 compare_reduce_fusion.17
  587.2 0.4 fusion.20
  587.7 0.7 compare_reduce_fusion.13
  591.6 0.7 compare_reduce_fusion.9
  594.9 0.6 compare_reduce_fusion.8
  595.5 0.7 compare_reduce_fusion.4
  599.4 0.1 reshape.723
  599.5 0.8 compare_reduce_fusion
  602.8 0.7 multiply_add_fusion.2
  603.6 0.7 reshape.724.picks
  604.3 12.2 %shard_map.102 = bf16[8,32,32,128]{3,2,1,0:T(8,128)(2,1)} custom-call(s32[256]{0:T(256)} %reshape.724.picks, bf16[1024,512]{1,0:T(8,128)(2,1)} %feats.1, bf16[3,512,512]{2,1,0:T(8,128)(2,1)} %bitcast.152, bf16[32,64,512]{2,1,0:T(8,128)(2,1)} %tiles.1), custom_call_target="tpu_custom_call" | custom-call | flops 2684354560 | bytes 7340032 | tf_op jit(solution)/shard_map/pallas_call | solution.py:447
  616.8 0.2 convolution_convert_fusion.3
  617.2 0.2 convolution_convert_fusion.1
  617.7 1.3 convert_reduce_fusion.2
  620.5 0.1 select_bitcast_fusion
  620.9 0.1 select_reduce_fusion.7
  621.7 0.2 constant_dynamic-update-slice_fusion.12
  621.9 0.2 convolution_convert_fusion.2
  622.1 0.2 convert_reduce_fusion.12
  622.4 0.2 select_reduce_fusion.5
  623.0 0.2 convert_reduce_fusion.1
  623.4 0.5 fusion.19
  623.9 0.2 select_reduce_fusion.1
  624.2 277.8 %conditional.1 = (bf16[2048,512]{1,0:T(8,128)(2,1)}) conditional(s32[]{:T(128)} %convert_element_type.95, (s32[32,1]{0,1:T(1,128)S(1)}, s32[32]{0:T(128)S(1)}, bf16[8,32,32,128]{3,2,1,0:T(8,128)(2,1)}, f32[2048]{0:T(1024)S(1)}, bf16[1024,512]{1,0:T(8,128)(2,1)S(1)}, /*index=5*/f32[512]{0:T(512)S(1)}) %tuple.116, (f32[2048]{0:T(1024)S(1)}, ...), branch_computations={%region_39.42_spmd, %region_42.43_spmd} | conditional | flops 3245388800 | bytes 198335008 | solution.py:531
  624.5 1.3 broadcast_in_dim.101.refs_4_
  625.8 276.1 %branch_1_fun.1 = bf16[32,64,512]{2,1,0:T(8,128)(2,1)} custom-call(s32[60]{0:T(128)S(1)} %get-tuple-element.40.refs_0_, s32[120]{0:T(128)S(1)} %get-tuple-element.41.refs_1_, s32[416]{0:T(512)S(1)} %get-tuple-element.42.refs_2_, bf16[8,32,32,128]{3,2,1,0:T(8,128)(2,1)} %get-tuple-element.43.refs_3_, f32[32,64,128]{2,1,0:T(8,128)} %broadcast_in_dim.101.refs_4_, ...), custom_call_target="tpu_custom_call" | custom-call | tf_op jit(solution)/shard_map/cond/branch_1_fun/pallas_call | solution.py:466
  902.0 3.0 copy.148
  (101 shorter events, 4.3 us)
Async XLA Ops:
  604.3 12.2 %copy-start.1 = (s32[2048]{0:T(1024)S(1)}, s32[2048]{0:T(1024)}, u32[]{:S(2)}) copy-start(s32[2048]{0:T(1024)} %param.19) | copy-start | bytes 24580
  616.5 7.6 copy-start
  616.5 7.6 copy-start.2
  616.6 7.6 copy-start.3
  616.6 7.6 copy-start.4

commit v2 on v1

--- a/solution.py
+++ b/solution.py
@@ -14,10 +14,12 @@
 LB = 32
 
 Z_LOCAL, Z_CAP = 12, (24, 20, 14, 6)
-X_LOCAL, X_CAP = 40, (40, 20)
-MERGE = 144
-Y_FAR = LB // 2
-Y_LIST = LB + Y_FAR
+X_LOCAL, X_CAP = 30, (32, 14)
+MERGE = 96
+Y_CAP = (24, 11)
+GROUP = LB // NX
+FAR = GROUP // 2
+R_LIST = GROUP + FAR
 
 COLS = 128
 HEIGHT = 32
@@ -39,6 +41,7 @@
 
 Z_RIGHT, Z_LEFT, Z_SLOTS = bases(Z_LOCAL, Z_CAP, 0)
 X_RIGHT, X_LEFT, X_SLOTS = bases(X_LOCAL, X_CAP, 1)
+Y_RIGHT, Y_LEFT, Y_SLOTS = bases(LB, Y_CAP, 1)
 
 
 def tri(n):
@@ -95,8 +98,9 @@
     sz, sx, sy = number // (NX * NY), (number // NY) % NX, number % NY
     mz, mx, my = me // (NX * NY), (me // NY) % NX, me % NY
 
+    home, spare = block // GROUP, dx * GROUP + block % GROUP
     grid = lambda a: lax.dynamic_index_in_dim(a.reshape(NZ, NX, NY, -1), my, 2, keepdims=False)
-    gz, gx, gy, gb = grid(dz), grid(dx), grid(dy), grid(block)
+    gz, gx, gy, gb = grid(dz), grid(home), grid(dy), grid(spare)
     z_delta = (gz - jnp.arange(NZ)[:, None, None]) % NZ
     z_addr, z_which, z_place = listed(z_delta, NZ, len(Z_CAP), Z_RIGHT, Z_LEFT, 0)
     mine = lambda a: lax.dynamic_index_in_dim(
@@ -119,27 +123,26 @@
         (X_LOCAL, X_CAP[0], X_CAP[0]),
     )
 
+    holder = (dz * (NX * NY) + home * NY + sy[:, None]).reshape(1, -1)
+    wanted = (((dy - sy[:, None]) % NY) * LB + spare).reshape(1, -1)
+    n_targets = NY * LB
+    holds = (holder == number[:, None]).astype(jnp.bfloat16)
+    wants = (wanted == jnp.arange(n_targets)[:, None]).astype(jnp.bfloat16)
+    contract = (((1,), (1,)), ((), ()))
+    hists = lax.dot_general(holds, wants, contract, preferred_element_type=jnp.float32)
+    hists = hists.astype(jnp.int32)
+    line_hists = lax.dynamic_slice_in_dim(hists, mz * (NX * NY) + mx * NY, NY, 0)
+    hist = lax.dynamic_index_in_dim(line_hists, my, 0, keepdims=False)
+    y_delta = jnp.where(line_hists > 0, (jnp.arange(n_targets) // LB)[None, :], NY)
+    y_addr, y_which, y_place = listed(y_delta, NY, len(Y_CAP), Y_RIGHT, Y_LEFT, 1)
+    seen = lambda a: lax.dynamic_index_in_dim(a, my, 0, keepdims=False)
+    start = jnp.sum(jnp.where(tri(n_targets).T > 0, hist[None, :], 0), axis=1)
+    last = jnp.where(hist > 0, start + hist - 1, MERGE)
+    y_lists = table(last, hist > 0, seen(y_which), seen(y_place), (0, Y_CAP[0], Y_CAP[0]))
+
     arrived = (here & (lx == mx)).reshape(-1)
-    y_delta = (lines(gy).reshape(-1) - my) % NY
-    lb = lines(gb).reshape(-1)
-    target = jnp.where(
-        y_delta == 0,
-        lb,
-        jnp.where(
-            y_delta == 1,
-            LB + Y_FAR + lb,
-            jnp.where(
-                y_delta == 3,
-                LB + Y_LIST + Y_FAR + lb,
-                jnp.where(lb < Y_FAR, LB + lb, LB + Y_LIST + lb - Y_FAR),
-            ),
-        ),
-    )
-    n_targets = LB + 2 * Y_LIST
+    target = ((lines(gy).reshape(-1) - my) % NY) * LB + lines(gb).reshape(-1)
     onehot = (target[None, :] == jnp.arange(n_targets)[:, None]) & arrived[None, :]
-    hist = jnp.sum(onehot.astype(jnp.int32), axis=1)
-    earlier = jnp.arange(n_targets)[None, :] < jnp.arange(n_targets)[:, None]
-    start = jnp.sum(jnp.where(earlier, hist[None, :], 0), axis=1)
     rank = before(onehot)
     spot = jnp.sum(jnp.where(onehot, rank + start[:, None], 0), axis=0)
     seat = jnp.arange(MERGE)[:, None]
@@ -150,7 +153,13 @@
     y_first = jnp.sum(
         ((start[None, :] == seat) & (hist > 0)[None, :]).astype(jnp.int32), axis=1
     )
-    y_last = jnp.where(hist > 0, start + hist - 1, MERGE)
+    finals = []
+    for hop in range(1, NY):
+        source = (my + NY - hop) % NY
+        there = lax.dynamic_index_in_dim(y_addr, source, 0, keepdims=False)
+        count = lax.dynamic_index_in_dim(line_hists, source, 0, keepdims=False)
+        span = slice(hop * LB, (hop + 1) * LB)
+        finals.append(jnp.where(count[span] > 0, there[span], 0))
 
     def ring_fits(counts, local, caps):
         ring = counts.shape[0]
@@ -168,31 +177,65 @@
     all_z = (dz - sz[:, None]) % NZ
     z_counts = jnp.stack([jnp.sum((all_z == k).astype(jnp.int32), axis=1) for k in range(NZ)])
     fits = ring_fits(z_counts, Z_LOCAL, Z_CAP)
-    holder = (dz * NX * NY + (sx * NY + sy)[:, None]).reshape(1, -1)
-    holds = (holder == number[:, None]).astype(jnp.bfloat16)
-    goes = (((dx - sx[:, None]) % NX).reshape(1, -1) == jnp.arange(NX)[:, None]).astype(jnp.bfloat16)
-    x_counts = lax.dot_general(
-        goes, holds, (((1,), (1,)), ((), ())), preferred_element_type=jnp.float32
-    ).astype(jnp.int32)
-    fits &= ring_fits(x_counts, X_LOCAL, X_CAP)
-    by_x = x_counts.reshape(NX, NZ, NX, NY)
-    for dest in range(NX):
-        total = sum(by_x[(dest - at) % NX, :, at, :] for at in range(NX))
-        fits &= jnp.all(total <= MERGE)
-    y_tab = jnp.concatenate([y_src, y_first, y_last]).astype(jnp.int32)
+    keeper = (dz * (NX * NY) + (sx * NY + sy)[:, None]).reshape(1, -1)
+    keeps = (keeper == number[:, None]).astype(jnp.bfloat16)
+    goes = (((home - sx[:, None]) % NX).reshape(1, -1) == jnp.arange(NX)[:, None]).astype(jnp.bfloat16)
+    x_counts = lax.dot_general(goes, keeps, contract, preferred_element_type=jnp.float32)
+    fits &= ring_fits(x_counts.astype(jnp.int32), X_LOCAL, X_CAP)
+    fits &= jnp.all(jnp.sum(hists, axis=1) <= MERGE)
+    y_counts = jnp.sum((hists > 0).astype(jnp.int32).reshape(ROWS, NY, LB), axis=2).T
+    fits &= ring_fits(y_counts, LB, Y_CAP)
+    y_tab = jnp.concatenate([y_src, y_first, last[:LB], y_lists] + finals).astype(jnp.int32)
     return z_tab, x_tab, y_tab, fits
 
 
-def partials_kernel(picks, feats, weight, tiles, out, msgs):
+def partials_kernel(picks, key, feats, weight, tiles, out, keys, msgs, send, recv):
+    me = lax.axis_index("rows")
+    mz, mx, my = me // (NX * NY), (me // NY) % NX, me % NY
+
+    def at(z, x, y):
+        return {"rows": (z % NZ) * (NX * NY) + (x % NX) * NY + y % NY}
+
+    hops = [at(mz + k, mx, my) for k in range(1, NZ)]
+    hops += [at(mz, mx + k, my) for k in range(1, NX)]
+    hops += [at(mz, mx, my + k) for k in range(1, NY)]
+    barrier = pltpu.get_barrier_semaphore()
+    for device in hops:
+        pl.semaphore_signal(barrier, inc=1, device_id=device, device_id_type=MESH)
+
+    def copies(first, n, src, dst):
+        return [
+            pltpu.make_async_remote_copy(
+                src_ref=src, dst_ref=dst, send_sem=send.at[i], recv_sem=recv.at[i],
+                device_id=hops[i], device_id_type=MESH,
+            )
+            for i in range(first, first + n)
+        ]
+
+    along_z = copies(0, NZ - 1, key, keys.at[my, mx, mz])
+    along_x = copies(NZ - 1, NX - 1, keys.at[my, mx], keys.at[my, mx])
+    along_y = copies(NZ + NX - 2, NY - 1, keys.at[my], keys.at[my])
+
+    def begin(items):
+        for item in items:
+            item.start()
+
+    def landed(items):
+        for item in items:
+            item.wait_recv()
+
+    keys[my, mx, mz] = key[...]
     n_rel, per = weight.shape[0], feats.shape[0] // TILE
     step = 256
-    for r in range(n_rel):
+
+    def messages(r):
         for s in range(feats.shape[0] // step):
             m = jnp.dot(
                 feats[s * step : (s + 1) * step, :], weight[r], preferred_element_type=jnp.float32
             ).astype(jnp.bfloat16)
-            at = r * per + s * (step // TILE)
-            msgs[at : at + step // TILE] = m.reshape(step // TILE, TILE, m.shape[1])
+            spot = r * per + s * (step // TILE)
+            msgs[spot : spot + step // TILE] = m.reshape(step // TILE, TILE, m.shape[1])
+
     kt = tiles.shape[2] // TILE
 
     def one(p, carry):
@@ -205,17 +248,35 @@
                 ]
         return carry
 
-    lax.fori_loop(0, tiles.shape[0], one, 0)
+    parts = tiles.shape[0]
+    messages(0)
+    pl.semaphore_wait(barrier, len(hops))
+    begin(along_z)
+    for r in range(1, n_rel):
+        messages(r)
+    lax.fori_loop(0, parts // 4, one, 0)
+    landed(along_z)
+    begin(along_x)
+    lax.fori_loop(parts // 4, 5 * parts // 8, one, 0)
+    landed(along_x)
+    begin(along_y)
+    lax.fori_loop(5 * parts // 8, parts, one, 0)
+    landed(along_y)
+    for item in along_z + along_x + along_y:
+        item.wait_send()
 
 
 def schedule():
-    unit = 1.41 * 2 / CHUNKS / 2
-    rings = {
+    unit = 1.58 / CHUNKS
+    links = {"z": "z", "x": "x", "y": "y", "r": "x"}
+    sends = {
         "z": [c * unit for c in Z_CAP],
         "x": [c * unit for c in X_CAP],
-        "y": [Y_LIST * unit, Y_FAR * unit],
+        "y": [c * unit for c in Y_CAP],
+        "r": [R_LIST * unit, FAR * unit],
     }
-    work = {"z": 1.0, "x": 1.0, "y": 3.5, "f": 1.5, "g": 1.5}
+    stages = ["z", "x", "y", "r", "g"]
+    work = {"z": 0.5, "x": 0.5, "y": 1.2, "r": 0.7, "g": 1.2}
     free = {"z": 0.0, "x": 0.0, "y": 0.0, "h": 0.0}
     now, order = 0.0, []
     ready = {("z", 0, c): 0.0 for c in range(CHUNKS)}
@@ -225,24 +286,25 @@
             start = max(t, now)
             if kind == "z" and k == 0:
                 start = max(start, free["z"] - 2.5)
-            rank = (start, 0 if k > 0 else 1, c)
+            rank = (start, 0 if k > 0 else 1, c, -stages.index(kind))
             if best is None or rank < best[0]:
                 best = (rank, (kind, k, c), start)
         _, (kind, k, c), start = best
         del ready[(kind, k, c)]
         order.append((kind, k, c))
         now = start + (work[kind] if k == 0 else 0.1)
-        if kind in rings:
-            sends = rings[kind]
-            if k < len(sends):
-                free[kind] = max(free[kind], now) + sends[k]
-                ready[(kind, k + 1, c)] = free[kind] + 1.8
-            if k == len(sends):
-                follow = {"z": "x", "x": "y", "y": "f"}[kind]
-                ready[(follow, 0, c)] = now
-        elif kind == "f":
+        if kind == "g":
+            continue
+        if k < len(sends[kind]):
+            link = links[kind]
+            free[link] = max(free[link], now) + sends[kind][k]
+            ready[(kind, k + 1, c)] = free[link] + 1.8
+        elif kind == "r":
+            now += 0.7
             free["h"] = max(free["h"], now) + 0.8
             ready[("g", 0, c)] = free["h"] + 1.0
+        else:
+            ready[(stages[stages.index(kind) + 1], 0, c)] = now
     return order
 
 
@@ -254,10 +316,13 @@
     xs = [next(it) for _ in range(CHUNKS)]
     xb = [next(it) for _ in range(CHUNKS)]
     ys = [next(it) for _ in range(CHUNKS)]
-    yr = [next(it) for _ in range(CHUNKS)]
+    yb = [next(it) for _ in range(CHUNKS)]
+    rs = [next(it) for _ in range(CHUNKS)]
+    rb = [next(it) for _ in range(CHUNKS)]
     ag = [next(it) for _ in range(CHUNKS)]
     stage, total = next(it), next(it)
-    z_send, z_recv, x_send, x_recv, y_send, y_recv, h_send, h_recv = [next(it) for _ in range(8)]
+    z_sems, x_sems, y_sems, r_sems = [(next(it), next(it)) for _ in range(4)]
+    h_send, h_recv = next(it), next(it)
 
     me, half = lax.axis_index("rows"), lax.axis_index("half")
     mz, mx, my = me // (NX * NY), (me // NY) % NX, me % NY
@@ -289,41 +354,20 @@
             device_id=device, device_id_type=MESH,
         )
 
-    def z_copies(c, k):
-        n = Z_CAP[k]
-        result = []
-        for side, device, base in ((0, zp, Z_RIGHT), (1, zm, Z_LEFT)):
-            if k == 0:
-                src = zs[c].at[pl.ds(side * n, n)]
-            else:
-                src = zb[c].at[pl.ds(base[k - 1], n)]
-            dst = zb[c].at[pl.ds(base[k], n)]
-            result.append(copy(src, dst, z_send.at[c, k, side], z_recv.at[c, k, side], device))
-        return result
-
-    def x_copies(c, k):
-        n = X_CAP[k]
-        result = []
-        for side, device, base in ((0, xp, X_RIGHT), (1, xm, X_LEFT)):
-            if k == 0:
-                src = xs[c].at[pl.ds(side * n, n)]
-            else:
-                src = xb[c].at[pl.ds(base[k - 1], n)]
-            dst = xb[c].at[pl.ds(base[k], n)]
-            result.append(copy(src, dst, x_send.at[c, k, side], x_recv.at[c, k, side], device))
-        return result
-
-    def y_copies(c, k):
-        result = []
-        for side, device in ((0, yp), (1, ym)):
-            if k == 0:
-                src = ys[c].at[pl.ds(LB + side * Y_LIST, Y_LIST)]
-                dst = yr[c].at[pl.ds(side * Y_LIST, Y_LIST)]
-            else:
-                src = yr[c].at[pl.ds(side * Y_LIST, Y_FAR)]
-                dst = yr[c].at[pl.ds(2 * Y_LIST + side * Y_FAR, Y_FAR)]
-            result.append(copy(src, dst, y_send.at[c, k, side], y_recv.at[c, k, side], device))
-        return result
+    def hop_copies(sent, held, sems, forward, backward, caps, right, left):
+        def copies(c, k):
+            n = caps[k]
+            result = []
+            for side, device, base in ((0, forward, right), (1, backward, left)):
+                if k == 0:
+                    src = sent[c].at[pl.ds(side * n, n)]
+                else:
+                    src = held[c].at[pl.ds(base[k - 1], n)]
+                dst = held[c].at[pl.ds(base[k], n)]
+                result.append(copy(src, dst, sems[0].at[c, k, side], sems[1].at[c, k, side], device))
+            return result
+
+        return copies, len(caps)
 
     def h_copy(c):
         return copy(ag[c].at[half], ag[c].at[half], h_send.at[c], h_recv.at[c], other)
@@ -331,8 +375,15 @@
     stage[MERGE] = jnp.zeros(stage.shape[1:], stage.dtype)
     for c in range(CHUNKS):
         xb[c][0] = jnp.zeros(xb[c].shape[1:], xb[c].dtype)
-
-    ring = {"z": (z_copies, len(Z_CAP)), "x": (x_copies, len(X_CAP)), "y": (y_copies, 2)}
+        yb[c][0] = jnp.zeros(yb[c].shape[1:], yb[c].dtype)
+
+    ring = {
+        "z": hop_copies(zs, zb, z_sems, zp, zm, Z_CAP, Z_RIGHT, Z_LEFT),
+        "x": hop_copies(xs, xb, x_sems, xp, xm, X_CAP, X_RIGHT, X_LEFT),
+        "y": hop_copies(ys, yb, y_sems, yp, ym, Y_CAP, Y_RIGHT, Y_LEFT),
+        "r": hop_copies(rs, rb, r_sems, xp, xm, (R_LIST, FAR), (0, 2 * R_LIST), (R_LIST, 2 * R_LIST + FAR)),
+    }
+    y_at = [2 * MERGE, 2 * MERGE + LB, 2 * MERGE + LB + 2 * Y_CAP[0]]
 
     for kind, k, c in order:
         row, col = c // COL_CHUNKS, c % COL_CHUNKS
@@ -343,16 +394,34 @@
             if k < hops:
                 for item in copies(c, k):
                     item.start()
+            elif kind == "r":
+
+                def finish(base, first, n):
+                    def body(i, carry):
+                        b = first + i
+                        v = rb[c][base + i].astype(jnp.float32)
+                        v = v / degree[b, row * HEIGHT : (row + 1) * HEIGHT, :]
+                        ag[c][half, b] = v.astype(jnp.bfloat16)
+                        return carry
+
+                    lax.fori_loop(0, n, body, 0, unroll=4)
+
+                far = 2 * R_LIST
+                finish(far + 2 * FAR, mx * GROUP, GROUP)
+                finish(FAR, (mx + NX - 1) % NX * GROUP, GROUP)
+                finish(R_LIST + FAR, (mx + 1) % NX * GROUP, GROUP)
+                finish(far, (mx + 2) % NX * GROUP, GROUP)
+                h_copy(c).start()
         elif kind == "z":
             read = lambda i: part[c, i]
             gather(zs[c], 0, read, z_tab, Z_LOCAL, 2 * Z_CAP[0])
-            for item in z_copies(c, 0):
+            for item in ring["z"][0](c, 0):
                 item.start()
             gather(zb[c], 0, read, z_tab, 0, Z_LOCAL)
         elif kind == "x":
             read = lambda i: zb[c][i]
             gather(xs[c], 0, read, x_tab, X_LOCAL, 2 * X_CAP[0])
-            for item in x_copies(c, 0):
+            for item in ring["x"][0](c, 0):
                 item.start()
             gather(xb[c], 1, read, x_tab, 0, X_LOCAL)
         elif kind == "y":
@@ -365,22 +434,32 @@
 
             lax.fori_loop(0, MERGE, add, jnp.zeros((HEIGHT, COLS), jnp.float32), unroll=4)
             read = lambda i: stage[i]
-            gather(ys[c], LB, read, y_tab, 2 * MERGE + LB, 2 * Y_LIST)
-            for item in y_copies(c, 0):
+            gather(ys[c], 0, read, y_tab, y_at[1], 2 * Y_CAP[0])
+            for item in ring["y"][0](c, 0):
                 item.start()
-            gather(ys[c], 0, read, y_tab, 2 * MERGE, LB)
-        elif kind == "f":
-
-            def finish(b, carry):
-                v = ys[c][b].astype(jnp.float32) + yr[c][Y_FAR + b].astype(jnp.float32)
-                v = v + yr[c][Y_LIST + Y_FAR + b].astype(jnp.float32)
-                v = v + yr[c][2 * Y_LIST + b].astype(jnp.float32)
-                v = v / degree[b, row * HEIGHT : (row + 1) * HEIGHT, :]
-                ag[c][half, b] = v.astype(jnp.bfloat16)
-                return carry
-
-            lax.fori_loop(0, LB, finish, 0, unroll=2)
-            h_copy(c).start()
+            gather(yb[c], 1, read, y_tab, y_at[0], LB)
+        elif kind == "r":
+
+            def collect(dst, base, hop, first, n):
+                group = (mx + hop) % NX * GROUP + first
+
+                def body(i, carry):
+                    q = group + i
+                    v = yb[c][1 + q].astype(jnp.float32)
+                    for other_y in range(NY - 1):
+                        v = v + yb[c][y_tab[y_at[2] + other_y * LB + q]].astype(jnp.float32)
+                    dst[base + i] = v.astype(dst.dtype)
+                    return carry
+
+                lax.fori_loop(0, n, body, 0, unroll=4)
+
+            collect(rs[c], 0, 2, 0, FAR)
+            collect(rs[c], FAR, 1, 0, GROUP)
+            collect(rs[c], R_LIST, 2, FAR, FAR)
+            collect(rs[c], R_LIST + FAR, NX - 1, 0, GROUP)
+            for item in ring["r"][0](c, 0):
+                item.start()
+            collect(rb[c], 2 * R_LIST + 2 * FAR, 0, 0, GROUP)
         else:
             h_copy(c).wait_recv()
             some = 8
@@ -442,20 +521,25 @@
     n_src_blocks = src_dev // tile
     n_local = in_degree.shape[0] // tile
 
-    keys = lax.all_gather(owner[:, 0] * LB + local_blk, "rows", axis=0, tiled=False)
+    key = jnp.zeros((8, 128), jnp.int32).at[0, :parts].set(owner[:, 0] * LB + local_blk)
     picks = (rel_id * n_src_blocks + src_blk).reshape(-1)
-    part = pl.pallas_call(
+    n_hops = NZ + NX + NY - 3
+    part, keys = pl.pallas_call(
         partials_kernel,
-        out_shape=jax.ShapeDtypeStruct((CHUNKS, parts, HEIGHT, COLS), jnp.bfloat16),
-        in_specs=[smem(), vmem(), vmem(), vmem()],
-        out_specs=vmem(),
-        scratch_shapes=[pltpu.VMEM((n_rel * n_src_blocks, tile, half_w), jnp.bfloat16)],
-        cost_estimate=pl.CostEstimate(
-            flops=2 * half_w * half_w * (src_dev * n_rel + parts * tile),
-            bytes_accessed=7 << 20,
-            transcendentals=0,
+        out_shape=(
+            jax.ShapeDtypeStruct((CHUNKS, parts, HEIGHT, COLS), jnp.bfloat16),
+            jax.ShapeDtypeStruct((NY, NX, NZ, 8, 128), jnp.int32),
         ),
-    )(picks, source_feats, rel_weight[:, 0], tiles)
+        in_specs=[smem(), vmem(), vmem(), vmem(), vmem()],
+        out_specs=(vmem(), vmem()),
+        scratch_shapes=[
+            pltpu.VMEM((n_rel * n_src_blocks, tile, half_w), jnp.bfloat16),
+            pltpu.SemaphoreType.DMA((n_hops,)),
+            pltpu.SemaphoreType.DMA((n_hops,)),
+        ],
+        compiler_params=pltpu.CompilerParams(collective_id=1, has_side_effects=True),
+    )(picks, key, source_feats, rel_weight[:, 0], tiles)
+    keys = keys[:, :, :, 0, :parts].transpose(2, 1, 0, 3).reshape(n_rows, parts)
     z_tab, x_tab, y_tab, fits = tables(keys, lax.axis_index("rows"))
     degree = in_degree.astype(jnp.float32)
 
@@ -472,8 +556,10 @@
             + block(Z_SLOTS)
             + block(2 * X_CAP[0])
             + block(X_SLOTS)
-            + block(LB + 2 * Y_LIST)
-            + block(2 * Y_LIST + 2 * Y_FAR)
+            + block(2 * Y_CAP[0])
+            + block(Y_SLOTS)
+            + block(2 * R_LIST)
+            + block(2 * R_LIST + 2 * FAR + GROUP)
             + [pltpu.VMEM((2, n_local, HEIGHT, COLS), jnp.bfloat16)] * CHUNKS
             + [
                 pltpu.VMEM((MERGE + 1, HEIGHT, COLS), jnp.bfloat16),
@@ -482,6 +568,8 @@
                 dma((CHUNKS, len(Z_CAP), 2)),
                 dma((CHUNKS, len(X_CAP), 2)),
                 dma((CHUNKS, len(X_CAP), 2)),
+                dma((CHUNKS, len(Y_CAP), 2)),
+                dma((CHUNKS, len(Y_CAP), 2)),
                 dma((CHUNKS, 2, 2)),
                 dma((CHUNKS, 2, 2)),
                 dma((CHUNKS,)),

time: 906 us -> 216 us (0.24)
  blocking collectives: 583 us -> 0 us
  Pallas kernels: 288 us -> 178 us
    unnamed x1 -> x0, blocking collectives: 583 us -> none
    pallas_call x1, Pallas kernels: 276 us -> 152 us  [routed(): pl.pallas_call(functools.partial(route_kernel, schedule()), out_shape=jax...]
    pallas_call x1, Pallas kernels: 12.2 us -> 26.2 us  [local(): pl.pallas_call(partials_kernel, out_shape=(jax.ShapeDtypeStruct((CHUNKS,...]
where the time goes in v2:
time: 216 us
  Pallas kernels  178 us (82%)
  between operations  13.3 us (6%)
  other arithmetic  12.5 us (6%)
  local copies, waits for them, and re-layouts  9.26 us (4%)
  matrix products  2.72 us (1%)
    pallas_call x1, Pallas kernels, routed(): pl.pallas_call(functools.partial(route_kernel, schedule()), out_shape=jax...  152 us
    pallas_call x1, Pallas kernels, local(): pl.pallas_call(partials_kernel, out_shape=(jax.ShapeDtypeStruct((CHUNKS,...  26.2 us

profile of v2, /device:TPU:1, one launch (start us, length us, event | category | flops | bytes accessed | tf_op | source)
XLA Modules:
  0.0 216.0 jit_solution(16550218394719010592)
XLA Ops:
  0.0 0.7 multiply_add_fusion.2
  0.8 0.7 reshape.1019.picks
  1.5 0.7 fusion.146
  2.1 0.6 scatter.4.key
  2.7 26.2 %shard_map.102 = (bf16[8,32,32,128]{3,2,1,0:T(8,128)(2,1)}, s32[4,4,8,8,128]{4,3,2,1,0:T(8,128)}) custom-call(s32[256]{0:T(256)} %reshape.1019.picks, s32[8,128]{1,0:T(8,128)} %scatter.4.key, bf16[1024,512]{1,0:T(8,128)(2,1)} %feats.1, bf16[3,512,512]{2,1,0:T(8,128)(2,1)} %bitcast.258, bf16[32,64,512]{2,1,0:T(8,128)(2,1)} %tiles.1), custom_call_target="tpu_custom_call" | custom-call | tf_op jit(solution)/shard_map/pallas_call | solution.py:527
  28.9 1.1 slice.189
  30.0 0.2 negate_select_fusion.2
  30.2 2.3 %convert_reduce_fusion.2 = (s32[8,4,4]{0,1,2:T(4,128)S(1)}, s32[8,4,4]{0,1,2:T(4,128)S(1)}, s32[8,4,4]{0,1,2:T(4,128)S(1)}, s32[8,4,4]{0,1,2:T(4,128)S(1)}, s32[...) fusion(s32[8,4,4,32]{3,0,1,2:T(8,128)S(1)} %get-tuple-element.174), kind=kLoop, calls=%fused_computation.83 | loop fusion | flops 97280 | bytes 20480 | tf_op jit(solution)/shard_map/reduce_sum | solution.py:178
  32.5 0.8 fusion.93
  36.5 0.7 fusion.94
  40.5 0.4 fusion.22
  40.9 0.6 compare_reduce_fusion.17
  41.6 0.7 compare_reduce_fusion.13
  45.5 0.8 fusion.171
  46.3 0.6 compare_reduce_fusion.12
  47.7 0.6 compare_reduce_fusion.11
  48.4 0.7 compare_reduce_fusion.7
  52.4 0.1 broadcast_compare_fusion.2
  52.7 0.2 convolution_convert_fusion.3
  53.2 0.2 convolution_convert_fusion.1
  53.6 0.7 convert_reduce_fusion.1
  56.0 0.2 constant_dynamic-update-slice_fusion.12
  56.2 0.2 convolution_convert_fusion.2
  56.4 0.2 convert_reduce_fusion.11
  57.0 0.1 select_add_fusion
  57.6 0.5 fusion.20
  58.1 0.2 select_reduce_fusion.1
  58.7 0.2 convert_reduce_fusion.12
  59.5 153.4 %conditional.1 = (bf16[2048,512]{1,0:T(8,128)(2,1)}) conditional(s32[]{:T(128)} %convert_element_type.124, (s32[32,1]{0,1:T(1,128)S(1)}, s32[32]{0:T(128)S(1)}, bf16[8,32,32,128]{3,2,1,0:T(8,128)(2,1)}, f32[2048]{0:T(1024)S(1)}, bf16[1024,512]{1,0:T(8,128)(2,1)S(1)}, /*index=5*/f32[512]{0:T(512)S(1)}) %tuple.147, (f32[2048]{0:T(1024)S(1)}, ...), branch_computations={%region_45.48_spmd, %region_48.49_spmd} | conditional | flops 3245388800 | bytes 198335008 | solution.py:619
  59.8 1.3 broadcast_in_dim.139.refs_4_
  61.1 151.8 %branch_1_fun.1 = bf16[32,64,512]{2,1,0:T(8,128)(2,1)} custom-call(s32[60]{0:T(128)S(1)} %get-tuple-element.52.refs_0_, s32[94]{0:T(128)S(1)} %get-tuple-element.53.refs_1_, s32[368]{0:T(512)S(1)} %get-tuple-element.54.refs_2_, bf16[8,32,32,128]{3,2,1,0:T(8,128)(2,1)} %get-tuple-element.55.refs_3_, f32[32,64,128]{2,1,0:T(8,128)} %broadcast_in_dim.139.refs_4_, ...), custom_call_target="tpu_custom_call" | custom-call | tf_op jit(solution)/shard_map/cond/branch_1_fun/pallas_call | solution.py:550
  212.9 3.0 %copy.226 = bf16[2048,512]{1,0:T(8,128)(2,1)} copy(bf16[2048,512]{1,0:T(8,128)(2,1)} %get-tuple-element.63) | data formatting | bytes 4194304
  (116 shorter events, 5.1 us)
Async XLA Ops:
  2.7 49.6 %copy-start.1 = (s32[2048]{0:T(1024)S(1)}, s32[2048]{0:T(1024)}, u32[]{:S(2)}) copy-start(s32[2048]{0:T(1024)} %param.21) | copy-start | bytes 24580
  40.9 18.6 %copy-start = (bf16[1024,512]{1,0:T(8,128)(2,1)S(1)}, bf16[1024,512]{1,0:T(8,128)(2,1)}, u32[]{:S(2)}) copy-start(bf16[1024,512]{1,0:T(8,128)(2,1)} %param.22) | copy-start | bytes 3145732
  40.9 18.6 %copy-start.2 = (f32[512]{0:T(512)S(1)}, f32[512]{0:T(512)}, u32[]{:S(2)}) copy-start(f32[512]{0:T(512)} %param.23) | copy-start | bytes 6148
  40.9 18.6 %copy-start.3 = (s32[32]{0:T(128)S(1)}, s32[32]{0:T(128)}, u32[]{:S(2)}) copy-start(s32[32]{0:T(128)} %param.20) | copy-start | bytes 388
  40.9 18.6 %copy-start.4 = (s32[32,1]{0,1:T(1,128)S(1)}, s32[32,1]{0,1:T(1,128)}, u32[]{:S(2)}) copy-start(s32[32,1]{0,1:T(1,128)} %param.19) | copy-start | bytes 388

commit v3 on v2

v3 whole, which is shorter than its diff:
```python
import functools

import jax
import jax.numpy as jnp
from jax import lax
from jax.experimental import pallas as pl
from jax.experimental.pallas import tpu as pltpu
from jax.sharding import PartitionSpec as P

MESH = pl.DeviceIdType.MESH
NZ, NX, NY = 8, 4, 4
ROWS = NZ * NX * NY
TILE = 64
LB = 32

Z_LOCAL, Z_CAP = 12, (24, 20, 14, 6)
X_LOCAL, X_CAP = 32, (34, 15)
MERGE = 96
Y_CAP = (26, 12)
GROUP = LB // NX
FAR = GROUP // 2
R_LIST = GROUP + FAR

COLS = 128
HEIGHT = 32
COL_CHUNKS = 4
ROW_CHUNKS = TILE // HEIGHT
CHUNKS = COL_CHUNKS * ROW_CHUNKS


def bases(local, caps, start):
    right, left, at = [], [], start + local
    for cap in caps:
        right.append(at)
        at += cap
    for cap in caps:
        left.append(at)
        at += cap
    return right, left, at


Z_RIGHT, Z_LEFT, Z_SLOTS = bases(Z_LOCAL, Z_CAP, 0)
X_RIGHT, X_LEFT, X_SLOTS = bases(X_LOCAL, X_CAP, 1)
Y_RIGHT, Y_LEFT, Y_SLOTS = bases(LB, Y_CAP, 1)


def ones_where(mask):
    return jnp.where(mask, 1.0, 0.0).astype(jnp.bfloat16)


def iota(shape, axis):
    return lax.broadcasted_iota(jnp.int32, shape, axis)


def dot32(a, b, transposed=False):
    dims = (((1,), (1 if transposed else 0,)), ((), ()))
    v = lax.dot_general(
        a.astype(jnp.bfloat16), b.astype(jnp.bfloat16), dims, preferred_element_type=jnp.float32
    )
    return v.astype(jnp.int32)


def tables(k, me):
    mz, mx, my = me // (NX * NY), (me // NY) % NX, me % NY
    n, seg = 128, LB
    wide = (n, n)
    low, col = iota(wide, 0), iota(wide, 1)
    same = (low // seg) == (col // seg)
    tri_all = ones_where(low < col)
    tri_seg = ones_where((low < col) & same)
    sum_seg = ones_where(same)
    shape = k.shape
    lane, row = iota(shape, 1), iota(shape, 0)
    owner, block = k // LB, k % LB
    dz, dy = owner // (NX * NY), owner % NY
    home, spare = block // GROUP, (owner // NY) % NX * GROUP + block % GROUP
    sz, sy, sx, p = row % NZ, row // NZ, lane // seg, lane % seg

    def number(mask):
        return jnp.where(mask, 1, 0)

    def listed(delta, ring, starts, right_base, left_base, local_base, before, total):
        half = ring // 2
        odd = before([delta == half])[0] % 2
        to_right = ((delta >= 1) & (delta < half)) | ((delta == half) & (odd == 0))
        to_left = ((delta > half) & (delta < ring)) | ((delta == half) & (odd == 1))
        dist = jnp.where(delta <= half, delta, ring - delta)
        masks = [delta == 0]
        masks += [to_right & (dist == h) for h in range(1, half + 1)]
        masks += [to_left & (dist == h) for h in range(1, half + 1)]
        ranks, totals = before(masks), total(masks)
        address = jnp.where(masks[0], local_base + ranks[0], 0)
        slot = jnp.where(masks[0], starts[0] + ranks[0], n)
        worst = []
        for side, base in ((0, right_base), (1, left_base)):
            farther = jnp.zeros_like(totals[0])
            for h in range(half, 0, -1):
                at = 1 + side * half + h - 1
                address = jnp.where(masks[at], base[h - 1] + farther + ranks[at], address)
                slot = jnp.where(masks[at], starts[1 + side] + farther + ranks[at], slot)
                farther = farther + totals[at]
                worst.append((h - 1, farther))
        return address, slot, totals[0], worst

    def stacked(masks, matrix):
        v = dot32(jnp.concatenate([ones_where(m) for m in masks], axis=0), matrix)
        rows = masks[0].shape[0]
        return [v[i * rows : (i + 1) * rows] for i in range(len(masks))]

    def overflow(kept, local, worst, caps):
        bad = number(kept > local)
        for h, count in worst:
            bad = bad | number(count > caps[h])
        return bad

    z_addr, z_slot, z_kept, z_worst = listed(
        (dz + NZ - sz) % NZ, NZ, (0, Z_LOCAL, Z_LOCAL + Z_CAP[0]), Z_RIGHT, Z_LEFT, 0,
        lambda m: stacked(m, tri_seg), lambda m: stacked(m, sum_seg),
    )
    bad = overflow(z_kept, Z_LOCAL, z_worst, Z_CAP)

    def placed(values, slots, valid):
        hit = ones_where(jnp.broadcast_to(jnp.where(valid, slots, n), wide) == low)
        return dot32(values, hit, True)

    def pick(a, index, count):
        total = jnp.zeros_like(a[:1])
        for i in range(count):
            total = jnp.where(index == i, a[i : i + 1], total)
        return total

    def pick_y(a):
        total = jnp.zeros_like(a[:NZ])
        for i in range(NY):
            total = jnp.where(my == i, a[i * NZ : (i + 1) * NZ], total)
        return total

    lane8 = iota((NZ, n), 1)
    own = pick(pick_y(z_slot), mz, NZ)
    z_tab = placed(lane8[:1] % seg, own, lane8[:1] // seg == mx)

    def before_x(masks):
        inner, whole = stacked(masks, tri_seg), stacked(masks, sum_seg)
        r, c = iota((NZ, NZ), 0), iota((NZ, NZ), 1)
        lower = ones_where(c < r)
        groups = masks[0].shape[0] // NZ
        outer = [
            jnp.concatenate([dot32(lower, w[g * NZ : (g + 1) * NZ]) for g in range(groups)], axis=0)
            for w in whole
        ]
        return [a + b for a, b in zip(inner, outer)]

    def total_x(masks):
        whole = stacked(masks, sum_seg)
        groups = masks[0].shape[0] // NZ
        return [
            jnp.concatenate(
                [
                    jnp.broadcast_to(
                        jnp.sum(w[g * NZ : (g + 1) * NZ], axis=0, keepdims=True), (NZ, n)
                    )
                    for g in range(groups)
                ],
                axis=0,
            )
            for w in whole
        ]

    dz8, home8, dy8, spare8 = pick_y(dz), pick_y(home), pick_y(dy), pick_y(spare)
    here = dz8 == mz
    x_addr, x_slot, _, _ = listed(
        jnp.where(here, (home8 + NX - lane8 // seg) % NX, NX), NX,
        (0, X_LOCAL, X_LOCAL + X_CAP[0]), X_RIGHT, X_LEFT, 1, before_x, total_x,
    )
    z_addr8 = pick_y(z_addr)
    x_tab = jnp.zeros((1, n), jnp.int32)
    for z in range(NZ):
        x_tab = x_tab + placed(
            z_addr8[z : z + 1], x_slot[z : z + 1], here[z : z + 1] & (lane8[:1] // seg == mx)
        )
    for z in range(NZ):
        deltas = [(dz == z) & ((home + NX - sx) % NX == d) for d in range(NX)]
        kept, right, tied, left = total_x(deltas)
        near, far = tied // 2, (tied + 1) // 2
        bad = bad | overflow(kept, X_LOCAL, [(1, far), (0, far + right), (0, near + left)], X_CAP)

    spots = dz * NX + home
    wanted = (dy + NY - sy) % NY * LB + spare
    hists = []
    holder = iota((NZ * NX, n), 0)
    for y in range(NY):
        total = jnp.zeros((NZ * NX, n), jnp.int32)
        for z in range(NZ):
            r = y * NZ + z
            holds = ones_where(jnp.broadcast_to(spots[r : r + 1], (NZ * NX, n)) == holder)
            wants = ones_where(jnp.broadcast_to(wanted[r : r + 1], wide) == low)
            total = total + dot32(holds, wants, True)
        hists.append(total)
        count = jnp.sum(total, axis=1, keepdims=True)
        bad = bad | number(jnp.broadcast_to(count, total.shape) > MERGE)
        present = dot32(ones_where(total > 0), sum_seg)
        group = iota(total.shape, 1) // seg
        tied = present
        bad = bad | number((group == 1) & (present > Y_CAP[0]))
        bad = bad | number((group == 3) & (present > Y_CAP[0]))
        bad = bad | number((group == 2) & ((present + 1) // 2 > Y_CAP[1]))
        ties = ones_where((total > 0) & (group == 2))
        every = dot32(ties, jnp.ones(wide, jnp.bfloat16))
        bad = bad | number((group == 1) & (present + (every + 1) // 2 > Y_CAP[0]))
        bad = bad | number((group == 3) & (present + every // 2 > Y_CAP[0]))
    index = mz * NX + mx
    lines = []
    for y in range(NY):
        mine = iota((NZ * NX, n), 0) == index
        lines.append(jnp.sum(jnp.where(mine, hists[y], 0), axis=0, keepdims=True))
    pad = [jnp.zeros((1, n), jnp.int32)] * (NZ - NY)
    line = jnp.concatenate(lines + pad, axis=0)
    ones_all = jnp.ones(wide, jnp.bfloat16)
    y_addr, y_slot, _, _ = listed(
        jnp.where(line > 0, lane8 // seg, NY), NY, (n, 0, Y_CAP[0]), Y_RIGHT, Y_LEFT, 1,
        lambda m: stacked(m, tri_all), lambda m: stacked(m, ones_all),
    )
    hist = pick(line, my, NY)
    start = dot32(hist, tri_all)
    last = jnp.where(hist > 0, start + hist - 1, MERGE)
    y_lists = placed(last, pick(y_slot, my, NY), hist > 0)
    finals = jnp.zeros((1, n), jnp.int32)
    for hop in range(1, NY):
        source = (my + NY - hop) % NY
        there = jnp.where(pick(line, source, NY) > 0, pick(y_addr, source, NY), 0)
        finals = jnp.where(lane8[:1] // seg == hop, there, finals)

    arrived = here & (home8 == mx)
    wanted8 = (dy8 + NY - my) % NY * LB + spare8
    y_src = jnp.zeros((1, n), jnp.int32)
    y_first = jnp.zeros((1, n), jnp.int32)
    ahead = start
    for z in range(NZ):
        valid = arrived[z : z + 1]
        hot = ones_where(jnp.broadcast_to(jnp.where(valid, wanted8[z : z + 1], n), wide) == low)
        inner = dot32(hot, tri_all)
        rank = jnp.sum(jnp.where(hot > 0, inner, 0), axis=0, keepdims=True)
        seat = dot32(ahead, hot) + rank
        first = ones_where(seat == dot32(start, hot))
        y_src = y_src + placed(x_addr[z : z + 1], seat, valid)
        y_first = y_first + placed(first, seat, valid)
        ahead = ahead + dot32(jnp.ones((1, n), jnp.bfloat16), hot, True)
    flag = jnp.max(bad.astype(jnp.float32), axis=(0, 1), keepdims=True).astype(jnp.int32)
    flag = jnp.broadcast_to(flag, (1, n))
    z_tab = jnp.minimum(z_tab, seg - 1)
    x_tab = jnp.minimum(x_tab, Z_SLOTS - 1)
    y_src = jnp.minimum(y_src, X_SLOTS - 1)
    last = jnp.minimum(last, MERGE)
    y_lists = jnp.minimum(y_lists, MERGE)
    finals = jnp.minimum(finals, Y_SLOTS - 1)
    return jnp.concatenate([z_tab, x_tab, y_src, y_first, last, y_lists, finals, flag], axis=0)


def messages(r, feats, weight, msgs):
    step, per = 256, feats.shape[0] // TILE
    for s in range(feats.shape[0] // step):
        m = jnp.dot(
            feats[s * step : (s + 1) * step, :], weight[r], preferred_element_type=jnp.float32
        ).astype(jnp.bfloat16)
        spot = r * per + s * (step // TILE)
        msgs[spot : spot + step // TILE] = m.reshape(step // TILE, TILE, m.shape[1])


def partial_of(p, picks, tiles, msgs):
    kt = tiles.shape[2] // TILE
    rhs = jnp.concatenate([msgs[picks[p * kt + k]] for k in range(kt)], axis=0)
    return jnp.dot(tiles[p], rhs, preferred_element_type=jnp.float32).astype(jnp.bfloat16)


def partials_kernel(picks, feats, weight, tiles, out, msgs):
    for r in range(weight.shape[0]):
        messages(r, feats, weight, msgs)

    def one(p, carry):
        out[p] = partial_of(p, picks, tiles, msgs)
        return carry

    lax.fori_loop(0, tiles.shape[0], one, 0)


def schedule():
    unit = 1.58 / CHUNKS
    links = {"z": "z", "x": "x", "y": "y", "r": "x"}
    sends = {
        "z": [c * unit for c in Z_CAP],
        "x": [c * unit for c in X_CAP],
        "y": [c * unit for c in Y_CAP],
        "r": [R_LIST * unit, FAR * unit],
    }
    stages = ["z", "x", "y", "r", "g"]
    work = {"z": 0.5, "x": 0.5, "y": 1.2, "r": 0.7, "g": 1.2}
    free = {"z": 0.0, "x": 0.0, "y": 0.0, "h": 0.0}
    now, order = 0.0, []
    ready = {("z", 0, c): 0.0 for c in range(CHUNKS)}
    begun = 0
    while ready:
        best = None
        for (kind, k, c), t in ready.items():
            start = max(t, now)
            if kind == "z" and k == 0:
                start = max(start, free["z"] - 2.5)
            rank = (start, 0 if k > 0 else 1, c, -stages.index(kind))
            if best is None or rank < best[0]:
                best = (rank, (kind, k, c), start)
        _, (kind, k, c), start = best
        del ready[(kind, k, c)]
        order.append((kind, k, c))
        begun += (kind, k) == ("z", 0)
        if begun == 2:
            order.append(("t", 0, 0))
            start, begun = start + 5.0, 3
        now = start + (work[kind] if k == 0 else 0.1)
        if kind == "g":
            continue
        if k < len(sends[kind]):
            link = links[kind]
            free[link] = max(free[link], now) + sends[kind][k]
            ready[(kind, k + 1, c)] = free[link] + 1.8
        elif kind == "r":
            now += 0.7
            free["h"] = max(free["h"], now) + 0.8
            ready[("g", 0, c)] = free["h"] + 1.0
        else:
            ready[(stages[stages.index(kind) + 1], 0, c)] = now
    return order


def rings(me):
    mz, mx, my = me // (NX * NY), (me // NY) % NX, me % NY

    def at(z, x, y):
        return {"rows": (z % NZ) * (NX * NY) + (x % NX) * NY + y % NY}

    along_z = [at(mz + k, mx, my) for k in range(1, NZ)]
    along_x = [at(mz, mx + k, my) for k in range(1, NX)]
    along_y = [at(mz, mx, my + k) for k in range(1, NY)]
    return mz, mx, my, along_z, along_x, along_y


def copy(src, dst, send, recv, device):
    return pltpu.make_async_remote_copy(
        src_ref=src, dst_ref=dst, send_sem=send, recv_sem=recv,
        device_id=device, device_id_type=MESH,
    )


def front_kernel(picks, key, feats, weight, tiles, part, tab, msgs, keys, k_send, k_recv):
    me = lax.axis_index("rows")
    mz, mx, my, to_z, to_x, to_y = rings(me)
    hops = to_z + to_x + to_y
    barrier = pltpu.get_barrier_semaphore()
    for device in hops:
        pl.semaphore_signal(barrier, inc=1, device_id=device, device_id_type=MESH)

    def key_copies(first, n, src, dst):
        return [
            copy(src, dst, k_send.at[i], k_recv.at[i], hops[i]) for i in range(first, first + n)
        ]

    along_z = key_copies(0, NZ - 1, key, keys.at[my, mx, mz])
    along_x = key_copies(NZ - 1, NX - 1, keys.at[my, mx], keys.at[my, mx])
    along_y = key_copies(NZ + NX - 2, NY - 1, keys.at[my], keys.at[my])

    def begin(items):
        for item in items:
            item.start()

    def landed(items):
        for item in items:
            item.wait_recv()

    keys[my, mx, mz] = key[...]
    messages(0, feats, weight, msgs)
    pl.semaphore_wait(barrier, len(hops))
    begin(along_z)
    for r in range(1, weight.shape[0]):
        messages(r, feats, weight, msgs)

    def one(p, carry):
        v = partial_of(p, picks, tiles, msgs)
        for i in range(ROW_CHUNKS):
            for j in range(COL_CHUNKS):
                part[i * COL_CHUNKS + j, p] = v[
                    i * HEIGHT : (i + 1) * HEIGHT, j * COLS : (j + 1) * COLS
                ]
        return carry

    parts = tiles.shape[0]
    lax.fori_loop(0, parts // 4, one, 0)
    landed(along_z)
    begin(along_x)
    lax.fori_loop(parts // 4, 5 * parts // 8, one, 0)
    landed(along_x)
    begin(along_y)
    lax.fori_loop(5 * parts // 8, parts, one, 0)
    landed(along_y)

    def add_up(y):
        def body(i, held):
            return held + keys[y, i // NZ, i % NZ]

        return lax.fori_loop(0, NX * NZ, body, jnp.zeros((8, 128), jnp.int32), unroll=4)

    tab[...] = tables(jnp.concatenate([add_up(y) for y in range(NY)], axis=0), me)
    for item in along_z + along_x + along_y:
        item.wait_send()


def route_kernel(order, *refs):
    it = iter(refs)
    tab, part, counts, mix, bias, out = [next(it) for _ in range(6)]
    zs = [next(it) for _ in range(CHUNKS)]
    zb = [next(it) for _ in range(CHUNKS)]
    xs = [next(it) for _ in range(CHUNKS)]
    xb = [next(it) for _ in range(CHUNKS)]
    ys = [next(it) for _ in range(CHUNKS)]
    yb = [next(it) for _ in range(CHUNKS)]
    rs = [next(it) for _ in range(CHUNKS)]
    rb = [next(it) for _ in range(CHUNKS)]
    ag = [next(it) for _ in range(CHUNKS)]
    stage, total, degree = next(it), next(it), next(it)
    z_sems, x_sems, y_sems, r_sems = [(next(it), next(it)) for _ in range(4)]
    h_send, h_recv = next(it), next(it)

    me, half = lax.axis_index("rows"), lax.axis_index("half")
    mz, mx, my, to_z, to_x, to_y = rings(me)
    zp, zm, xp, xm, yp, ym = to_z[0], to_z[-1], to_x[0], to_x[-1], to_y[0], to_y[-1]
    other = {"half": 1 - half}
    barrier = pltpu.get_barrier_semaphore()
    neighbours = (zp, zm, xp, xm, yp, ym, other)
    for device in neighbours:
        pl.semaphore_signal(barrier, inc=1, device_id=device, device_id_type=MESH)
    pl.semaphore_wait(barrier, len(neighbours))

    def gather(dst, base, read, entry, n):
        def body(j, carry):
            dst[base + j] = read(entry(j))
            return carry

        lax.fori_loop(0, n, body, 0, unroll=4)

    def hop_copies(sent, held, sems, forward, backward, caps, right, left):
        def copies(c, k):
            n = caps[k]
            result = []
            for side, device, base in ((0, forward, right), (1, backward, left)):
                if k == 0:
                    src = sent[c].at[pl.ds(side * n, n)]
                else:
                    src = held[c].at[pl.ds(base[k - 1], n)]
                dst = held[c].at[pl.ds(base[k], n)]
                result.append(copy(src, dst, sems[0].at[c, k, side], sems[1].at[c, k, side], device))
            return result

        return copies, len(caps)

    def h_copy(c):
        return copy(ag[c].at[half], ag[c].at[half], h_send.at[c], h_recv.at[c], other)

    stage[MERGE] = jnp.zeros(stage.shape[1:], stage.dtype)
    for c in range(CHUNKS):
        xb[c][0] = jnp.zeros(xb[c].shape[1:], xb[c].dtype)
        yb[c][0] = jnp.zeros(yb[c].shape[1:], yb[c].dtype)

    ring = {
        "z": hop_copies(zs, zb, z_sems, zp, zm, Z_CAP, Z_RIGHT, Z_LEFT),
        "x": hop_copies(xs, xb, x_sems, xp, xm, X_CAP, X_RIGHT, X_LEFT),
        "y": hop_copies(ys, yb, y_sems, yp, ym, Y_CAP, Y_RIGHT, Y_LEFT),
        "r": hop_copies(rs, rb, r_sems, xp, xm, (R_LIST, FAR), (0, 2 * R_LIST), (R_LIST, 2 * R_LIST + FAR)),
    }
    Z_TAB, X_TAB, Y_SRC, Y_FIRST, LAST, LISTS, FINALS = range(7)

    for kind, k, c in order:
        row, col = c // COL_CHUNKS, c % COL_CHUNKS
        if kind == "t":
            eye = iota((128, 128), 0) == iota((128, 128), 1)
            per = 128 // TILE
            for i in range(LB // per):
                one_row = jnp.broadcast_to(counts[i : i + 1].astype(jnp.float32), (128, 128))
                spread = jnp.dot(
                    jnp.where(eye, one_row, 0.0).astype(jnp.bfloat16),
                    jnp.ones((128, COLS), jnp.bfloat16),
                    preferred_element_type=jnp.float32,
                )
                degree[i * per : (i + 1) * per] = spread.reshape(per, TILE, COLS)
        elif kind in ring and k > 0:
            copies, hops = ring[kind]
            for item in copies(c, k - 1):
                item.wait_recv()
            if k < hops:
                for item in copies(c, k):
                    item.start()
            elif kind == "r":

                def finish(base, first, n):
                    def body(i, carry):
                        b = first + i
                        v = rb[c][base + i].astype(jnp.float32)
                        v = v / degree[b, row * HEIGHT : (row + 1) * HEIGHT, :]
                        ag[c][half, b] = v.astype(jnp.bfloat16)
                        return carry

                    lax.fori_loop(0, n, body, 0, unroll=4)

                far = 2 * R_LIST
                finish(far + 2 * FAR, mx * GROUP, GROUP)
                finish(FAR, (mx + NX - 1) % NX * GROUP, GROUP)
                finish(R_LIST + FAR, (mx + 1) % NX * GROUP, GROUP)
                finish(far, (mx + 2) % NX * GROUP, GROUP)
                h_copy(c).start()
        elif kind == "z":
            read = lambda i: part[c, i]
            gather(zs[c], 0, read, lambda j: tab[Z_TAB, Z_LOCAL + j], 2 * Z_CAP[0])
            for item in ring["z"][0](c, 0):
                item.start()
            gather(zb[c], 0, read, lambda j: tab[Z_TAB, j], Z_LOCAL)
        elif kind == "x":
            read = lambda i: zb[c][i]
            gather(xs[c], 0, read, lambda j: tab[X_TAB, X_LOCAL + j], 2 * X_CAP[0])
            for item in ring["x"][0](c, 0):
                item.start()
            gather(xb[c], 1, read, lambda j: tab[X_TAB, j], X_LOCAL)
        elif kind == "y":

            def add(j, total_now):
                v = xb[c][tab[Y_SRC, j]].astype(jnp.float32)
                total_now = jnp.where(tab[Y_FIRST, j] > 0, v, total_now + v)
                stage[j] = total_now.astype(stage.dtype)
                return total_now

            lax.fori_loop(0, MERGE, add, jnp.zeros((HEIGHT, COLS), jnp.float32), unroll=4)
            read = lambda i: stage[i]
            gather(ys[c], 0, read, lambda j: tab[LISTS, j], 2 * Y_CAP[0])
            for item in ring["y"][0](c, 0):
                item.start()
            gather(yb[c], 1, read, lambda j: tab[LAST, j], LB)
        elif kind == "r":

            def collect(dst, base, hop, first, n):
                group = (mx + hop) % NX * GROUP + first

                def body(i, carry):
                    q = group + i
                    v = yb[c][1 + q].astype(jnp.float32)
                    for other_y in range(NY - 1):
                        v = v + yb[c][tab[FINALS, (other_y + 1) * LB + q]].astype(jnp.float32)
                    dst[base + i] = v.astype(dst.dtype)
                    return carry

                lax.fori_loop(0, n, body, 0, unroll=4)

            collect(rs[c], 0, 2, 0, FAR)
            collect(rs[c], FAR, 1, 0, GROUP)
            collect(rs[c], R_LIST, 2, FAR, FAR)
            collect(rs[c], R_LIST + FAR, NX - 1, 0, GROUP)
            for item in ring["r"][0](c, 0):
                item.start()
            collect(rb[c], 2 * R_LIST + 2 * FAR, 0, 0, GROUP)
        else:
            h_copy(c).wait_recv()
            some = 8
            width = mix.shape[0] // 2
            w = jnp.concatenate(
                [
                    mix[col * COLS : (col + 1) * COLS, :],
                    mix[width + col * COLS : width + (col + 1) * COLS, :],
                ],
                axis=0,
            )

            def mixing(b, carry):
                blocks = pl.ds(b * some, some)
                a = jnp.concatenate(
                    [
                        ag[c][0, blocks].reshape(some * HEIGHT, COLS),
                        ag[c][1, blocks].reshape(some * HEIGHT, COLS),
                    ],
                    axis=1,
                )
                v = jnp.dot(a, w, preferred_element_type=jnp.float32)
                v = v.reshape(some, HEIGHT, v.shape[1])
                if col > 0:
                    v = v + total[blocks]
                if col < COL_CHUNKS - 1:
                    total[blocks] = v
                else:
                    v = jnp.maximum(v + bias[...][None], 0.0)
                    out[blocks, row * HEIGHT : (row + 1) * HEIGHT, :] = v.astype(out.dtype)
                return carry

            lax.fori_loop(0, LB // some, mixing, 0)

    for c in range(CHUNKS):
        for copies, hops in ring.values():
            for k in range(hops):
                for item in copies(c, k):
                    item.wait_send()
        h_copy(c).wait_send()


def vmem():
    return pl.BlockSpec(memory_space=pltpu.VMEM)


def smem():
    return pl.BlockSpec(memory_space=pltpu.SMEM)


def local(
    source_feats, rel_weight, tiles, src_blk, rel_id, owner, local_blk, in_degree, mix_weight, bias
):
    n_rows = lax.axis_size("rows")
    src_dev, half_w = source_feats.shape
    tile = tiles.shape[1]
    parts, per_row = src_blk.shape
    n_rel = rel_weight.shape[0]
    n_src_blocks = src_dev // tile
    n_local = in_degree.shape[0] // tile

    me = lax.axis_index("rows")
    spot_z = lax.broadcasted_iota(jnp.int32, (NZ, 128), 0) == me // (NX * NY)
    spot_x = lax.broadcasted_iota(jnp.int32, (NZ, 128), 1) // LB == (me // NY) % NX
    own = jnp.tile(owner[:, 0] * LB + local_blk, 128 // parts)
    key = jnp.where(spot_z & spot_x, own[None, :], 0)
    weight = rel_weight.reshape(n_rel, half_w, half_w)
    picks = (rel_id * n_src_blocks + src_blk).reshape(-1)
    n_hops = NZ + NX + NY - 3
    degree = in_degree.astype(jnp.float32)
    block = lambda n: [pltpu.VMEM((n, HEIGHT, COLS), jnp.bfloat16)] * CHUNKS
    dma = pltpu.SemaphoreType.DMA
    pair = lambda n: [dma((CHUNKS, n, 2)), dma((CHUNKS, n, 2))]
    part, tab = pl.pallas_call(
        front_kernel,
        out_shape=(
            jax.ShapeDtypeStruct((CHUNKS, parts, HEIGHT, COLS), jnp.bfloat16),
            jax.ShapeDtypeStruct((8, 128), jnp.int32),
        ),
        in_specs=[smem()] + [vmem()] * 4,
        out_specs=(vmem(), vmem()),
        scratch_shapes=[
            pltpu.VMEM((n_rel * n_src_blocks, tile, half_w), jnp.bfloat16),
            pltpu.VMEM((NY, NX, NZ, 8, 128), jnp.int32),
            dma((n_hops,)),
            dma((n_hops,)),
        ],
        compiler_params=pltpu.CompilerParams(collective_id=1, has_side_effects=True),
    )(picks, key, source_feats, weight, tiles)

    def routed():
        out = pl.pallas_call(
            functools.partial(route_kernel, schedule()),
            out_shape=jax.ShapeDtypeStruct((n_local, tile, half_w), jnp.bfloat16),
            in_specs=[smem()] + [vmem()] * 4,
            out_specs=vmem(),
            scratch_shapes=block(2 * Z_CAP[0])
            + block(Z_SLOTS)
            + block(2 * X_CAP[0])
            + block(X_SLOTS)
            + block(2 * Y_CAP[0])
            + block(Y_SLOTS)
            + block(2 * R_LIST)
            + block(2 * R_LIST + 2 * FAR + GROUP)
            + [pltpu.VMEM((2, n_local, HEIGHT, COLS), jnp.bfloat16)] * CHUNKS
            + [
                pltpu.VMEM((MERGE + 1, HEIGHT, COLS), jnp.bfloat16),
                pltpu.VMEM((n_local, HEIGHT, half_w), jnp.float32),
                pltpu.VMEM((n_local, tile, COLS), jnp.float32),
            ]
            + pair(len(Z_CAP))
            + pair(len(X_CAP))
            + pair(len(Y_CAP))
            + pair(2)
            + [dma((CHUNKS,)), dma((CHUNKS,))],
            compiler_params=pltpu.CompilerParams(
                collective_id=0, has_side_effects=True, vmem_limit_bytes=67043328
            ),
        )(tab, part, in_degree.reshape(-1, 128), mix_weight, bias[None, :])
        return out.reshape(n_local * tile, half_w)

    def dense():
        partials = pl.pallas_call(
            partials_kernel,
            out_shape=jax.ShapeDtypeStruct((parts, tile, half_w), jnp.bfloat16),
            in_specs=[smem(), vmem(), vmem(), vmem()],
            out_specs=vmem(),
            scratch_shapes=[pltpu.VMEM((n_rel * n_src_blocks, tile, half_w), jnp.bfloat16)],
        )(picks, source_feats, weight, tiles).reshape(parts, tile * half_w)
        capacity = max(2, 2 * parts // n_rows)
        target_dev = owner[:, 0]
        positions = jnp.arange(parts, dtype=jnp.int32)
        earlier = (target_dev[:, None] == target_dev[None, :]) & (
            positions[None, :] < positions[:, None]
        )
        rank = jnp.sum(earlier.astype(jnp.int32), axis=1)
        slot = target_dev * capacity + rank
        slot_ids = jnp.arange(n_rows * capacity, dtype=jnp.int32)
        placing = slot_ids[:, None] == slot[None, :]
        outgoing = jnp.dot(
            placing.astype(jnp.bfloat16), partials, preferred_element_type=jnp.float32
        ).astype(jnp.bfloat16)
        out_ids = jnp.sum(jnp.where(placing, local_blk[None, :] + 1, 0), axis=1) - 1
        block_index = jnp.arange(n_local, dtype=jnp.int32)
        arrived = lax.all_to_all(outgoing, "rows", split_axis=0, concat_axis=0, tiled=True)
        arrived_ids = lax.all_to_all(out_ids, "rows", split_axis=0, concat_axis=0, tiled=True)
        selector = (arrived_ids[None, :] == block_index[:, None]).astype(jnp.bfloat16)
        summed = jnp.dot(selector, arrived, preferred_element_type=jnp.float32)
        summed = summed.reshape(n_local * tile, half_w)
        agg = (summed / degree[:, None]).astype(jnp.bfloat16)
        theirs = lax.ppermute(agg, "half", [(0, 1), (1, 0)])
        half = lax.axis_index("half")
        w_mine = lax.dynamic_slice_in_dim(mix_weight, half * half_w, half_w, 0)
        w_theirs = lax.dynamic_slice_in_dim(mix_weight, (1 - half) * half_w, half_w, 0)
        mixed = jnp.dot(
            jnp.concatenate([agg, theirs], axis=1),
            jnp.concatenate([w_mine, w_theirs], axis=0),
            preferred_element_type=jnp.float32,
        )
        return jax.nn.relu(mixed + bias).astype(jnp.bfloat16)

    return lax.cond(tab[7, 0] > 0, dense, routed)


def solution(mesh):
    placed = (
        P("rows", "half"),
        P(None, "half", None, None),
        P("rows", None, None),
        P("rows", None),
        P("rows", None),
        P("rows", None),
        P("rows"),
        P("rows"),
        P(None, "half"),
        P("half"),
    )
    return jax.shard_map(
        local, mesh=mesh, in_specs=placed, out_specs=P("rows", "half"), check_vma=False
    )
```

time: 216 us -> 198 us (0.917)
  between operations: 13.3 us -> 0.7 us
  Pallas kernels: 178 us -> 189 us
  other arithmetic: 12.5 us -> 3.37 us
  local copies, waits for them, and re-layouts: 9.26 us -> 4.5 us
  matrix products: 2.72 us -> 0 us
    pallas_call x1, Pallas kernels: 26.2 us -> 32.1 us  [local(): pl.pallas_call(front_kernel, out_shape=(jax.ShapeDtypeStruct((CHUNKS, par...]
    pallas_call x1, Pallas kernels: 152 us -> 157 us  [routed(): pl.pallas_call(functools.partial(route_kernel, schedule()), out_shape=jax...]
    reduce_and x7 -> x0, other arithmetic: 4.91 us -> none  [the longest x4 2.99 us: ring_fits(): ok &= jnp.all(far <= caps[k - 1])]
    reduce_sum x13 -> x0, other arithmetic: 4.35 us -> none  [the longest x1 2.29 us: tables(): jnp.sum((all_z == k).astype(jnp.int32), axis=1)]
    dot_general x9 -> x0, matrix products: 2.72 us -> none  [the longest x7 1.5 us: before(): counts = jnp.dot(flat, tri(shape[-1]), preferred_element_type=jnp.float32)]
where the time goes in v3:
time: 198 us
  Pallas kernels  189 us (95%)
  local copies, waits for them, and re-layouts  4.5 us (2%)
  other arithmetic  3.37 us (2%)
    pallas_call x1, Pallas kernels, routed(): pl.pallas_call(functools.partial(route_kernel, schedule()), out_shape=jax...  157 us
    pallas_call x1, Pallas kernels, local(): pl.pallas_call(front_kernel, out_shape=(jax.ShapeDtypeStruct((CHUNKS, par...  32.1 us

profile of v3, /device:TPU:1, one launch (start us, length us, event | category | flops | bytes accessed | tf_op | source)
XLA Modules:
  0.0 197.9 jit_solution(9249195116989198849)
XLA Ops:
  0.0 0.7 multiply_add_fusion.1
  0.7 0.1 copy.17
  0.8 0.1 reshape.57.picks
  0.9 0.7 bitcast_add_fusion
  1.6 0.1 broadcast_in_dim.36
  1.7 0.7 fusion.15.key
  2.4 32.1 %shard_map.102 = (bf16[8,32,32,128]{3,2,1,0:T(8,128)(2,1)}, s32[8,128]{1,0:T(8,128)}) custom-call(s32[256]{0:T(256)S(1)} %reshape.57.picks, s32[8,128]{1,0:T(8,128)} %fusion.15.key, bf16[1024,512]{1,0:T(8,128)(2,1)} %feats.1, bf16[3,512,512]{2,1,0:T(8,128)(2,1)} %bitcast.18, bf16[32,64,512]{2,1,0:T(8,128)(2,1)} %tiles.1), custom_call_target="tpu_custom_call" | custom-call | tf_op jit(solution)/shard_map/pallas_call | solution.py:637
  34.5 1.2 slice.3
  36.3 1.3 convert_element_type.25
  37.6 157.2 %conditional.1 = (bf16[2048,512]{1,0:T(8,128)(2,1)}) conditional(s32[]{:T(128)} %bitcast.7, (s32[2048]{0:T(1024)}, f32[512]{0:T(512)}, s32[8,128]{1,0:T(8,128)}, bf16[8,32,32,128]{3,2,1,0:T(8,128)(2,1)}, bf16[1024,512]{1,0:T(8,128)(2,1)}) %tuple.11, (s32[32,1]{0,1:T(1,128)}, s32[32]{0:T(128)}, s32[256]{0:T(256)S(1)}, bf16[1024,512]{1,0:T(8,128)(2,1)}, ...), branch_computations={%region_0.1_spmd, %region_1.4_spmd} | conditional | flops 3245388800 | bytes 198380192 | solution.py:725
  37.6 157.0 %branch_0_fun.1 = bf16[32,64,512]{2,1,0:T(8,128)(2,1)} custom-call(s32[8,128]{1,0:T(8,128)} %get-tuple-element.36.refs_0_, bf16[8,32,32,128]{3,2,1,0:T(8,128)(2,1)} %get-tuple-element.37.refs_1_, s32[16,128]{1,0:T(8,128)} %bitcast.refs_2_, bf16[1024,512]{1,0:T(8,128)(2,1)} %get-tuple-element.39.refs_3_, f32[1,512]{1,0:T(1,128)} %bitcast.20), custom_call_target="tpu_custom_call" | custom-call | tf_op jit(solution)/shard_map/cond/branch_0_fun/pallas_call | solution.py:655
  194.8 3.0 %copy.22 = bf16[2048,512]{1,0:T(8,128)(2,1)} copy(bf16[2048,512]{1,0:T(8,128)(2,1)} %get-tuple-element.54) | data formatting | bytes 4194304
  (4 shorter events, 0.0 us)

commit v4 on v3

--- a/solution.py
+++ b/solution.py
@@ -60,7 +60,7 @@
     return v.astype(jnp.int32)
 
 
-def tables(k, me):
+def tables(k, me, first_only=False):
     mz, mx, my = me // (NX * NY), (me // NY) % NX, me % NY
     n, seg = 128, LB
     wide = (n, n)
@@ -136,8 +136,10 @@
         return total
 
     lane8 = iota((NZ, n), 1)
-    own = pick(pick_y(z_slot), mz, NZ)
-    z_tab = placed(lane8[:1] % seg, own, lane8[:1] // seg == mx)
+    own = pick(z_slot if first_only else pick_y(z_slot), mz, NZ)
+    if first_only:
+        z_tab = placed(lane8[:1] % seg, own, lane8[:1] // seg == mx)
+        return jnp.broadcast_to(jnp.minimum(z_tab, seg - 1), (NZ, n))
 
     def before_x(masks):
         inner, whole = stacked(masks, tri_seg), stacked(masks, sum_seg)
@@ -247,13 +249,12 @@
         ahead = ahead + dot32(jnp.ones((1, n), jnp.bfloat16), hot, True)
     flag = jnp.max(bad.astype(jnp.float32), axis=(0, 1), keepdims=True).astype(jnp.int32)
     flag = jnp.broadcast_to(flag, (1, n))
-    z_tab = jnp.minimum(z_tab, seg - 1)
     x_tab = jnp.minimum(x_tab, Z_SLOTS - 1)
     y_src = jnp.minimum(y_src, X_SLOTS - 1)
     last = jnp.minimum(last, MERGE)
     y_lists = jnp.minimum(y_lists, MERGE)
     finals = jnp.minimum(finals, Y_SLOTS - 1)
-    return jnp.concatenate([z_tab, x_tab, y_src, y_first, last, y_lists, finals, flag], axis=0)
+    return jnp.concatenate([x_tab, y_src, y_first, last, y_lists, finals, flag, flag], axis=0)
 
 
 def messages(r, feats, weight, msgs):
@@ -283,137 +284,29 @@
     lax.fori_loop(0, tiles.shape[0], one, 0)
 
 
+ORDER = (
+    0, 1, 500, 10, 11, 20, 21, 30, 2, 3, 40, 100, 31, 12, 41, 110, 13, 101, 120, 22,
+    200, 23, 32, 111, 4, 33, 42, 5, 102, 121, 201, 210, 14, 43, 103, 15, 211, 112, 24, 220,
+    300, 221, 25, 301, 122, 34, 6, 113, 310, 202, 44, 104, 35, 320, 123, 16, 45, 105, 7, 114,
+    212, 26, 17, 115, 222, 203, 311, 302, 36, 400, 124, 204, 27, 46, 106, 213, 125, 37, 205, 47,
+    107, 214, 321, 215, 116, 223, 224, 117, 303, 225, 126, 206, 401, 304, 127, 207, 312, 305, 322, 314,
+    216, 315, 313, 402, 217, 324, 325, 226, 306, 323, 227, 307, 403, 404, 316, 405, 317, 326, 327, 406,
+    407,
+)
+
+
 def schedule():
-    unit = 1.58 / CHUNKS
-    links = {"z": "z", "x": "x", "y": "y", "r": "x"}
-    sends = {
-        "z": [c * unit for c in Z_CAP],
-        "x": [c * unit for c in X_CAP],
-        "y": [c * unit for c in Y_CAP],
-        "r": [R_LIST * unit, FAR * unit],
-    }
-    stages = ["z", "x", "y", "r", "g"]
-    work = {"z": 0.5, "x": 0.5, "y": 1.2, "r": 0.7, "g": 1.2}
-    free = {"z": 0.0, "x": 0.0, "y": 0.0, "h": 0.0}
-    now, order = 0.0, []
-    ready = {("z", 0, c): 0.0 for c in range(CHUNKS)}
-    begun = 0
-    while ready:
-        best = None
-        for (kind, k, c), t in ready.items():
-            start = max(t, now)
-            if kind == "z" and k == 0:
-                start = max(start, free["z"] - 2.5)
-            rank = (start, 0 if k > 0 else 1, c, -stages.index(kind))
-            if best is None or rank < best[0]:
-                best = (rank, (kind, k, c), start)
-        _, (kind, k, c), start = best
-        del ready[(kind, k, c)]
-        order.append((kind, k, c))
-        begun += (kind, k) == ("z", 0)
-        if begun == 2:
-            order.append(("t", 0, 0))
-            start, begun = start + 5.0, 3
-        now = start + (work[kind] if k == 0 else 0.1)
-        if kind == "g":
-            continue
-        if k < len(sends[kind]):
-            link = links[kind]
-            free[link] = max(free[link], now) + sends[kind][k]
-            ready[(kind, k + 1, c)] = free[link] + 1.8
-        elif kind == "r":
-            now += 0.7
-            free["h"] = max(free["h"], now) + 0.8
-            ready[("g", 0, c)] = free["h"] + 1.0
-        else:
-            ready[(stages[stages.index(kind) + 1], 0, c)] = now
-    return order
-
-
-def rings(me):
-    mz, mx, my = me // (NX * NY), (me // NY) % NX, me % NY
-
-    def at(z, x, y):
-        return {"rows": (z % NZ) * (NX * NY) + (x % NX) * NY + y % NY}
-
-    along_z = [at(mz + k, mx, my) for k in range(1, NZ)]
-    along_x = [at(mz, mx + k, my) for k in range(1, NX)]
-    along_y = [at(mz, mx, my + k) for k in range(1, NY)]
-    return mz, mx, my, along_z, along_x, along_y
-
-
-def copy(src, dst, send, recv, device):
-    return pltpu.make_async_remote_copy(
-        src_ref=src, dst_ref=dst, send_sem=send, recv_sem=recv,
-        device_id=device, device_id_type=MESH,
-    )
-
-
-def front_kernel(picks, key, feats, weight, tiles, part, tab, msgs, keys, k_send, k_recv):
-    me = lax.axis_index("rows")
-    mz, mx, my, to_z, to_x, to_y = rings(me)
-    hops = to_z + to_x + to_y
-    barrier = pltpu.get_barrier_semaphore()
-    for device in hops:
-        pl.semaphore_signal(barrier, inc=1, device_id=device, device_id_type=MESH)
-
-    def key_copies(first, n, src, dst):
-        return [
-            copy(src, dst, k_send.at[i], k_recv.at[i], hops[i]) for i in range(first, first + n)
-        ]
-
-    along_z = key_copies(0, NZ - 1, key, keys.at[my, mx, mz])
-    along_x = key_copies(NZ - 1, NX - 1, keys.at[my, mx], keys.at[my, mx])
-    along_y = key_copies(NZ + NX - 2, NY - 1, keys.at[my], keys.at[my])
-
-    def begin(items):
-        for item in items:
-            item.start()
-
-    def landed(items):
-        for item in items:
-            item.wait_recv()
-
-    keys[my, mx, mz] = key[...]
-    messages(0, feats, weight, msgs)
-    pl.semaphore_wait(barrier, len(hops))
-    begin(along_z)
-    for r in range(1, weight.shape[0]):
-        messages(r, feats, weight, msgs)
-
-    def one(p, carry):
-        v = partial_of(p, picks, tiles, msgs)
-        for i in range(ROW_CHUNKS):
-            for j in range(COL_CHUNKS):
-                part[i * COL_CHUNKS + j, p] = v[
-                    i * HEIGHT : (i + 1) * HEIGHT, j * COLS : (j + 1) * COLS
-                ]
-        return carry
-
-    parts = tiles.shape[0]
-    lax.fori_loop(0, parts // 4, one, 0)
-    landed(along_z)
-    begin(along_x)
-    lax.fori_loop(parts // 4, 5 * parts // 8, one, 0)
-    landed(along_x)
-    begin(along_y)
-    lax.fori_loop(5 * parts // 8, parts, one, 0)
-    landed(along_y)
-
-    def add_up(y):
-        def body(i, held):
-            return held + keys[y, i // NZ, i % NZ]
-
-        return lax.fori_loop(0, NX * NZ, body, jnp.zeros((8, 128), jnp.int32), unroll=4)
-
-    tab[...] = tables(jnp.concatenate([add_up(y) for y in range(NY)], axis=0), me)
-    for item in along_z + along_x + along_y:
-        item.wait_send()
-
-
-def route_kernel(order, *refs):
+    return [("zxyrgt"[n // 100], n // 10 % 10, n % 10) for n in ORDER]
+
+
+def within(index, size):
+    return jnp.minimum(jnp.maximum(index, 0), size - 1)
+
+
+def layer_kernel(order, *refs):
     it = iter(refs)
-    tab, part, counts, mix, bias, out = [next(it) for _ in range(6)]
+    picks, key, feats, weight, tiles, counts, mix, bias, out, flag = [next(it) for _ in range(10)]
+    msgs, part, keys, z_tab_vec, z_tab_all, tab_vec, tab_all = [next(it) for _ in range(7)]
     zs = [next(it) for _ in range(CHUNKS)]
     zb = [next(it) for _ in range(CHUNKS)]
     xs = [next(it) for _ in range(CHUNKS)]
@@ -425,17 +318,78 @@
     ag = [next(it) for _ in range(CHUNKS)]
     stage, total, degree = next(it), next(it), next(it)
     z_sems, x_sems, y_sems, r_sems = [(next(it), next(it)) for _ in range(4)]
-    h_send, h_recv = next(it), next(it)
+    h_send, h_recv, k_send, k_recv, tab_sem = [next(it) for _ in range(5)]
+    z_tab, tab = z_tab_all.at[0], tab_all
 
     me, half = lax.axis_index("rows"), lax.axis_index("half")
-    mz, mx, my, to_z, to_x, to_y = rings(me)
-    zp, zm, xp, xm, yp, ym = to_z[0], to_z[-1], to_x[0], to_x[-1], to_y[0], to_y[-1]
+    mz, mx, my = me // (NX * NY), (me // NY) % NX, me % NY
+
+    def at(z, x, y):
+        return {"rows": (z % NZ) * (NX * NY) + (x % NX) * NY + y % NY}
+
+    zp, zm = at(mz + 1, mx, my), at(mz + NZ - 1, mx, my)
+    xp, xm = at(mz, mx + 1, my), at(mz, mx + NX - 1, my)
+    yp, ym = at(mz, mx, my + 1), at(mz, mx, my + NY - 1)
     other = {"half": 1 - half}
+    hops = [at(mz + k, mx, my) for k in range(1, NZ)]
+    hops += [at(mz, mx + k, my) for k in range(1, NX)]
+    hops += [at(mz, mx, my + k) for k in range(1, NY)]
+
     barrier = pltpu.get_barrier_semaphore()
-    neighbours = (zp, zm, xp, xm, yp, ym, other)
-    for device in neighbours:
+    for device in hops + [other]:
         pl.semaphore_signal(barrier, inc=1, device_id=device, device_id_type=MESH)
-    pl.semaphore_wait(barrier, len(neighbours))
+
+    def key_copies(first, n, src, dst):
+        return [
+            copy(src, dst, k_send.at[i], k_recv.at[i], hops[i]) for i in range(first, first + n)
+        ]
+
+    def copy(src, dst, send, recv, device):
+        return pltpu.make_async_remote_copy(
+            src_ref=src, dst_ref=dst, send_sem=send, recv_sem=recv,
+            device_id=device, device_id_type=MESH,
+        )
+
+    along_z = key_copies(0, NZ - 1, key, keys.at[my, mx, mz])
+    along_x = key_copies(NZ - 1, NX - 1, keys.at[my, mx], keys.at[my, mx])
+    along_y = key_copies(NZ + NX - 2, NY - 1, keys.at[my], keys.at[my])
+
+    def begin(items):
+        for item in items:
+            item.start()
+
+    def landed(items):
+        for item in items:
+            item.wait_recv()
+
+    keys[my, mx, mz] = key[...]
+    z_tab_vec[...] = tables(key[...], me, True)
+    messages(0, feats, weight, msgs)
+    pl.semaphore_wait(barrier, len(hops) + 1)
+    begin(along_z)
+    z_tab_copy = pltpu.make_async_copy(z_tab_vec, z_tab_all, tab_sem.at[0])
+    z_tab_copy.start()
+    for r in range(1, weight.shape[0]):
+        messages(r, feats, weight, msgs)
+
+    def one(p, carry):
+        v = partial_of(p, picks, tiles, msgs)
+        for i in range(ROW_CHUNKS):
+            for j in range(COL_CHUNKS):
+                part[i * COL_CHUNKS + j, p] = v[
+                    i * HEIGHT : (i + 1) * HEIGHT, j * COLS : (j + 1) * COLS
+                ]
+        return carry
+
+    parts = tiles.shape[0]
+    lax.fori_loop(0, parts // 4, one, 0)
+    landed(along_z)
+    begin(along_x)
+    lax.fori_loop(parts // 4, 5 * parts // 8, one, 0)
+    landed(along_x)
+    begin(along_y)
+    lax.fori_loop(5 * parts // 8, parts, one, 0)
+    z_tab_copy.wait()
 
     def gather(dst, base, read, entry, n):
         def body(j, carry):
@@ -473,11 +427,24 @@
         "y": hop_copies(ys, yb, y_sems, yp, ym, Y_CAP, Y_RIGHT, Y_LEFT),
         "r": hop_copies(rs, rb, r_sems, xp, xm, (R_LIST, FAR), (0, 2 * R_LIST), (R_LIST, 2 * R_LIST + FAR)),
     }
-    Z_TAB, X_TAB, Y_SRC, Y_FIRST, LAST, LISTS, FINALS = range(7)
+    X_TAB, Y_SRC, Y_FIRST, LAST, LISTS, FINALS = range(6)
 
     for kind, k, c in order:
         row, col = c // COL_CHUNKS, c % COL_CHUNKS
         if kind == "t":
+            landed(along_y)
+
+            def add_up(y):
+                def body(i, held):
+                    return held + keys[y, i // NZ, i % NZ]
+
+                return lax.fori_loop(0, NX * NZ, body, jnp.zeros((8, 128), jnp.int32), unroll=4)
+
+            found = tables(jnp.concatenate([add_up(y) for y in range(NY)], axis=0), me)
+            tab_vec[...] = found
+            flag[...] = found
+            tab_copy = pltpu.make_async_copy(tab_vec, tab_all, tab_sem.at[1])
+            tab_copy.start()
             eye = iota((128, 128), 0) == iota((128, 128), 1)
             per = 128 // TILE
             for i in range(LB // per):
@@ -488,6 +455,7 @@
                     preferred_element_type=jnp.float32,
                 )
                 degree[i * per : (i + 1) * per] = spread.reshape(per, TILE, COLS)
+            tab_copy.wait()
         elif kind in ring and k > 0:
             copies, hops = ring[kind]
             for item in copies(c, k - 1):
@@ -515,30 +483,30 @@
                 h_copy(c).start()
         elif kind == "z":
             read = lambda i: part[c, i]
-            gather(zs[c], 0, read, lambda j: tab[Z_TAB, Z_LOCAL + j], 2 * Z_CAP[0])
+            gather(zs[c], 0, read, lambda j: within(z_tab[Z_LOCAL + j], parts), 2 * Z_CAP[0])
             for item in ring["z"][0](c, 0):
                 item.start()
-            gather(zb[c], 0, read, lambda j: tab[Z_TAB, j], Z_LOCAL)
+            gather(zb[c], 0, read, lambda j: within(z_tab[j], parts), Z_LOCAL)
         elif kind == "x":
             read = lambda i: zb[c][i]
-            gather(xs[c], 0, read, lambda j: tab[X_TAB, X_LOCAL + j], 2 * X_CAP[0])
+            gather(xs[c], 0, read, lambda j: within(tab[X_TAB, X_LOCAL + j], Z_SLOTS), 2 * X_CAP[0])
             for item in ring["x"][0](c, 0):
                 item.start()
-            gather(xb[c], 1, read, lambda j: tab[X_TAB, j], X_LOCAL)
+            gather(xb[c], 1, read, lambda j: within(tab[X_TAB, j], Z_SLOTS), X_LOCAL)
         elif kind == "y":
 
             def add(j, total_now):
-                v = xb[c][tab[Y_SRC, j]].astype(jnp.float32)
+                v = xb[c][within(tab[Y_SRC, j], X_SLOTS)].astype(jnp.float32)
                 total_now = jnp.where(tab[Y_FIRST, j] > 0, v, total_now + v)
                 stage[j] = total_now.astype(stage.dtype)
                 return total_now
 
             lax.fori_loop(0, MERGE, add, jnp.zeros((HEIGHT, COLS), jnp.float32), unroll=4)
             read = lambda i: stage[i]
-            gather(ys[c], 0, read, lambda j: tab[LISTS, j], 2 * Y_CAP[0])
+            gather(ys[c], 0, read, lambda j: within(tab[LISTS, j], MERGE + 1), 2 * Y_CAP[0])
             for item in ring["y"][0](c, 0):
                 item.start()
-            gather(yb[c], 1, read, lambda j: tab[LAST, j], LB)
+            gather(yb[c], 1, read, lambda j: within(tab[LAST, j], MERGE + 1), LB)
         elif kind == "r":
 
             def collect(dst, base, hop, first, n):
@@ -548,7 +516,7 @@
                     q = group + i
                     v = yb[c][1 + q].astype(jnp.float32)
                     for other_y in range(NY - 1):
-                        v = v + yb[c][tab[FINALS, (other_y + 1) * LB + q]].astype(jnp.float32)
+                        v = v + yb[c][within(tab[FINALS, (other_y + 1) * LB + q], Y_SLOTS)].astype(jnp.float32)
                     dst[base + i] = v.astype(dst.dtype)
                     return carry
 
@@ -601,6 +569,8 @@
                 for item in copies(c, k):
                     item.wait_send()
         h_copy(c).wait_send()
+    for item in along_z + along_x + along_y:
+        item.wait_send()
 
 
 def vmem():
@@ -634,53 +604,47 @@
     block = lambda n: [pltpu.VMEM((n, HEIGHT, COLS), jnp.bfloat16)] * CHUNKS
     dma = pltpu.SemaphoreType.DMA
     pair = lambda n: [dma((CHUNKS, n, 2)), dma((CHUNKS, n, 2))]
-    part, tab = pl.pallas_call(
-        front_kernel,
+    out, flag = pl.pallas_call(
+        functools.partial(layer_kernel, schedule()),
         out_shape=(
-            jax.ShapeDtypeStruct((CHUNKS, parts, HEIGHT, COLS), jnp.bfloat16),
+            jax.ShapeDtypeStruct((n_local, tile, half_w), jnp.bfloat16),
             jax.ShapeDtypeStruct((8, 128), jnp.int32),
         ),
-        in_specs=[smem()] + [vmem()] * 4,
+        in_specs=[smem()] + [vmem()] * 7,
         out_specs=(vmem(), vmem()),
         scratch_shapes=[
             pltpu.VMEM((n_rel * n_src_blocks, tile, half_w), jnp.bfloat16),
+            pltpu.VMEM((CHUNKS, parts, HEIGHT, COLS), jnp.bfloat16),
             pltpu.VMEM((NY, NX, NZ, 8, 128), jnp.int32),
-            dma((n_hops,)),
-            dma((n_hops,)),
-        ],
-        compiler_params=pltpu.CompilerParams(collective_id=1, has_side_effects=True),
-    )(picks, key, source_feats, weight, tiles)
-
-    def routed():
-        out = pl.pallas_call(
-            functools.partial(route_kernel, schedule()),
-            out_shape=jax.ShapeDtypeStruct((n_local, tile, half_w), jnp.bfloat16),
-            in_specs=[smem()] + [vmem()] * 4,
-            out_specs=vmem(),
-            scratch_shapes=block(2 * Z_CAP[0])
-            + block(Z_SLOTS)
-            + block(2 * X_CAP[0])
-            + block(X_SLOTS)
-            + block(2 * Y_CAP[0])
-            + block(Y_SLOTS)
-            + block(2 * R_LIST)
-            + block(2 * R_LIST + 2 * FAR + GROUP)
-            + [pltpu.VMEM((2, n_local, HEIGHT, COLS), jnp.bfloat16)] * CHUNKS
-            + [
-                pltpu.VMEM((MERGE + 1, HEIGHT, COLS), jnp.bfloat16),
-                pltpu.VMEM((n_local, HEIGHT, half_w), jnp.float32),
-                pltpu.VMEM((n_local, tile, COLS), jnp.float32),
-            ]
-            + pair(len(Z_CAP))
-            + pair(len(X_CAP))
-            + pair(len(Y_CAP))
-            + pair(2)
-            + [dma((CHUNKS,)), dma((CHUNKS,))],
-            compiler_params=pltpu.CompilerParams(
-                collective_id=0, has_side_effects=True, vmem_limit_bytes=67043328
-            ),
-        )(tab, part, in_degree.reshape(-1, 128), mix_weight, bias[None, :])
-        return out.reshape(n_local * tile, half_w)
+            pltpu.VMEM((8, 128), jnp.int32),
+            pltpu.SMEM((8, 128), jnp.int32),
+            pltpu.VMEM((8, 128), jnp.int32),
+            pltpu.SMEM((8, 128), jnp.int32),
+        ]
+        + block(2 * Z_CAP[0])
+        + block(Z_SLOTS)
+        + block(2 * X_CAP[0])
+        + block(X_SLOTS)
+        + block(2 * Y_CAP[0])
+        + block(Y_SLOTS)
+        + block(2 * R_LIST)
+        + block(2 * R_LIST + 2 * FAR + GROUP)
+        + [pltpu.VMEM((2, n_local, HEIGHT, COLS), jnp.bfloat16)] * CHUNKS
+        + [
+            pltpu.VMEM((MERGE + 1, HEIGHT, COLS), jnp.bfloat16),
+            pltpu.VMEM((n_local, HEIGHT, half_w), jnp.float32),
+            pltpu.VMEM((n_local, tile, COLS), jnp.float32),
+        ]
+        + pair(len(Z_CAP))
+        + pair(len(X_CAP))
+        + pair(len(Y_CAP))
+        + pair(2)
+        + [dma((CHUNKS,)), dma((CHUNKS,)), dma((n_hops,)), dma((n_hops,)), dma((2,))],
+        compiler_params=pltpu.CompilerParams(
+            collective_id=0, has_side_effects=True, vmem_limit_bytes=67043328
+        ),
+    )(picks, key, source_feats, weight, tiles, in_degree.reshape(-1, 128), mix_weight, bias[None, :])
+    out = out.reshape(n_local * tile, half_w)
 
     def dense():
         partials = pl.pallas_call(
@@ -722,7 +686,7 @@
         )
         return jax.nn.relu(mixed + bias).astype(jnp.bfloat16)
 
-    return lax.cond(tab[7, 0] > 0, dense, routed)
+    return lax.cond(flag[6, 0] > 0, dense, lambda: out)
 
 
 def solution(mesh):

time: 198 us -> 172 us (0.87)
  Pallas kernels: 189 us -> 164 us
    pallas_call x2 -> x1, Pallas kernels: 189 us -> 164 us  [local(): pl.pallas_call(functools.partial(layer_kernel, schedule()), out_shape=(ja...]
where the time goes in v4:
time: 172 us
  Pallas kernels  164 us (95%)
  local copies, waits for them, and re-layouts  5.07 us (3%)
  other arithmetic  2.77 us (2%)
    pallas_call x1, Pallas kernels, local(): pl.pallas_call(functools.partial(layer_kernel, schedule()), out_shape=(ja...  164 us

profile of v4, /device:TPU:1, one launch (start us, length us, event | category | flops | bytes accessed | tf_op | source)
XLA Modules:
  0.0 172.1 jit_solution(15203716877279891831)
XLA Ops:
  0.0 0.7 multiply_add_fusion.1
  0.7 0.1 copy.17
  0.8 0.7 reshape.60.refs_0_
  1.5 0.7 bitcast_add_fusion
  2.1 0.1 broadcast_in_dim.36
  2.3 0.7 fusion.15.refs_1_
  2.9 163.5 %shard_map.102 = (bf16[32,64,512]{2,1,0:T(8,128)(2,1)}, s32[8,128]{1,0:T(8,128)}) custom-call(s32[256]{0:T(256)} %reshape.60.refs_0_, s32[8,128]{1,0:T(8,128)} %fusion.15.refs_1_, bf16[1024,512]{1,0:T(8,128)(2,1)} %refs_2_.1, bf16[3,512,512]{2,1,0:T(8,128)(2,1)} %bitcast.17, bf16[32,64,512]{2,1,0:T(8,128)(2,1)} %refs_4_.1, s32[16,128]{1,0:T(8,128)} %bitcast.20, ...), custom_call_target="tpu_custom_call" | custom-call | tf_op jit(solution)/shard_map/pallas_call | solution.py:607
  166.5 1.2 slice.3
  168.3 0.7 convert_element_type.25
  169.0 3.0 %copy.22 = bf16[2048,512]{1,0:T(8,128)(2,1)} copy(bf16[2048,512]{1,0:T(8,128)(2,1)} %get-tuple-element.42) | data formatting | bytes 4194304
  (5 shorter events, 0.0 us)

commit v5 on v4

--- a/solution.py
+++ b/solution.py
@@ -11,6 +11,7 @@
 NZ, NX, NY = 8, 4, 4
 ROWS = NZ * NX * NY
 TILE = 64
+REL = 3
 LB = 32
 
 Z_LOCAL, Z_CAP = 12, (24, 20, 14, 6)
@@ -267,18 +268,19 @@
         msgs[spot : spot + step // TILE] = m.reshape(step // TILE, TILE, m.shape[1])
 
 
-def partial_of(p, picks, tiles, msgs):
+def partial_of(p, rel, src, tiles, msgs):
+    per = msgs.shape[0] // REL
     kt = tiles.shape[2] // TILE
-    rhs = jnp.concatenate([msgs[picks[p * kt + k]] for k in range(kt)], axis=0)
+    rhs = jnp.concatenate([msgs[within(rel[k, p] * per + src[k, p], REL * per)] for k in range(kt)], axis=0)
     return jnp.dot(tiles[p], rhs, preferred_element_type=jnp.float32).astype(jnp.bfloat16)
 
 
-def partials_kernel(picks, feats, weight, tiles, out, msgs):
+def partials_kernel(rel, src, feats, weight, tiles, out, msgs):
     for r in range(weight.shape[0]):
         messages(r, feats, weight, msgs)
 
     def one(p, carry):
-        out[p] = partial_of(p, picks, tiles, msgs)
+        out[p] = partial_of(p, rel, src, tiles, msgs)
         return carry
 
     lax.fori_loop(0, tiles.shape[0], one, 0)
@@ -305,7 +307,7 @@
 
 def layer_kernel(order, *refs):
     it = iter(refs)
-    picks, key, feats, weight, tiles, counts, mix, bias, out, flag = [next(it) for _ in range(10)]
+    rel, src, key, feats, weight, tiles, counts, mix, bias, out, flag = [next(it) for _ in range(11)]
     msgs, part, keys, z_tab_vec, z_tab_all, tab_vec, tab_all = [next(it) for _ in range(7)]
     zs = [next(it) for _ in range(CHUNKS)]
     zb = [next(it) for _ in range(CHUNKS)]
@@ -373,7 +375,7 @@
         messages(r, feats, weight, msgs)
 
     def one(p, carry):
-        v = partial_of(p, picks, tiles, msgs)
+        v = partial_of(p, rel, src, tiles, msgs)
         for i in range(ROW_CHUNKS):
             for j in range(COL_CHUNKS):
                 part[i * COL_CHUNKS + j, p] = v[
@@ -442,7 +444,7 @@
 
             found = tables(jnp.concatenate([add_up(y) for y in range(NY)], axis=0), me)
             tab_vec[...] = found
-            flag[...] = found
+            flag[0, 0] = jnp.max(found[6:7].astype(jnp.float32)).astype(jnp.int32)
             tab_copy = pltpu.make_async_copy(tab_vec, tab_all, tab_sem.at[1])
             tab_copy.start()
             eye = iota((128, 128), 0) == iota((128, 128), 1)
@@ -598,7 +600,6 @@
     own = jnp.tile(owner[:, 0] * LB + local_blk, 128 // parts)
     key = jnp.where(spot_z & spot_x, own[None, :], 0)
     weight = rel_weight.reshape(n_rel, half_w, half_w)
-    picks = (rel_id * n_src_blocks + src_blk).reshape(-1)
     n_hops = NZ + NX + NY - 3
     degree = in_degree.astype(jnp.float32)
     block = lambda n: [pltpu.VMEM((n, HEIGHT, COLS), jnp.bfloat16)] * CHUNKS
@@ -608,10 +609,10 @@
         functools.partial(layer_kernel, schedule()),
         out_shape=(
             jax.ShapeDtypeStruct((n_local, tile, half_w), jnp.bfloat16),
-            jax.ShapeDtypeStruct((8, 128), jnp.int32),
+            jax.ShapeDtypeStruct((1, 1), jnp.int32),
         ),
-        in_specs=[smem()] + [vmem()] * 7,
-        out_specs=(vmem(), vmem()),
+        in_specs=[smem(), smem()] + [vmem()] * 7,
+        out_specs=(vmem(), smem()),
         scratch_shapes=[
             pltpu.VMEM((n_rel * n_src_blocks, tile, half_w), jnp.bfloat16),
             pltpu.VMEM((CHUNKS, parts, HEIGHT, COLS), jnp.bfloat16),
@@ -643,17 +644,17 @@
         compiler_params=pltpu.CompilerParams(
             collective_id=0, has_side_effects=True, vmem_limit_bytes=67043328
         ),
-    )(picks, key, source_feats, weight, tiles, in_degree.reshape(-1, 128), mix_weight, bias[None, :])
+    )(rel_id.T, src_blk.T, key, source_feats, weight, tiles, in_degree.reshape(-1, 128), mix_weight, bias[None, :])
     out = out.reshape(n_local * tile, half_w)
 
     def dense():
         partials = pl.pallas_call(
             partials_kernel,
             out_shape=jax.ShapeDtypeStruct((parts, tile, half_w), jnp.bfloat16),
-            in_specs=[smem(), vmem(), vmem(), vmem()],
+            in_specs=[smem(), smem(), vmem(), vmem(), vmem()],
             out_specs=vmem(),
             scratch_shapes=[pltpu.VMEM((n_rel * n_src_blocks, tile, half_w), jnp.bfloat16)],
-        )(picks, source_feats, weight, tiles).reshape(parts, tile * half_w)
+        )(rel_id.T, src_blk.T, source_feats, weight, tiles).reshape(parts, tile * half_w)
         capacity = max(2, 2 * parts // n_rows)
         target_dev = owner[:, 0]
         positions = jnp.arange(parts, dtype=jnp.int32)
@@ -686,7 +687,7 @@
         )
         return jax.nn.relu(mixed + bias).astype(jnp.bfloat16)
 
-    return lax.cond(flag[6, 0] > 0, dense, lambda: out)
+    return lax.cond(flag[0, 0] > 0, dense, lambda: out)
 
 
 def solution(mesh):

time: 172 us -> 169 us (0.983)
  local copies, waits for them, and re-layouts: 5.07 us -> 3.13 us
where the time goes in v5:
time: 169 us
  Pallas kernels  163 us (96%)
  local copies, waits for them, and re-layouts  3.13 us (2%)
  other arithmetic  2.06 us (1%)
    pallas_call x1, Pallas kernels, local(): pl.pallas_call(functools.partial(layer_kernel, schedule()), out_shape=(ja...  163 us

profile of v5, /device:TPU:1, one launch (start us, length us, event | category | flops | bytes accessed | tf_op | source)
XLA Modules:
  0.0 169.0 jit_solution(8523269957984501891)
XLA Ops:
  0.0 0.7 bitcast_add_fusion
  0.7 0.1 broadcast_in_dim.36
  0.8 0.7 fusion.15.refs_2_
  1.5 163.1 %shard_map.102 = (bf16[32,64,512]{2,1,0:T(8,128)(2,1)}, s32[1,1]{1,0:T(1,128)}) custom-call(s32[8,32]{1,0:T(8,128)} %bitcast.25, s32[8,32]{1,0:T(8,128)} %bitcast.27, s32[8,128]{1,0:T(8,128)} %fusion.15.refs_2_, bf16[1024,512]{1,0:T(8,128)(2,1)} %refs_3_.1, bf16[3,512,512]{2,1,0:T(8,128)(2,1)} %bitcast.21, bf16[32,64,512]{2,1,0:T(8,128)(2,1)} %refs_5_.1, ...), custom_call_target="tpu_custom_call" | custom-call | tf_op jit(solution)/shard_map/pallas_call | solution.py:608
  165.2 0.7 convert_element_type.25
  165.9 3.0 %copy.19 = bf16[2048,512]{1,0:T(8,128)(2,1)} copy(bf16[2048,512]{1,0:T(8,128)(2,1)} %get-tuple-element.45) | data formatting | bytes 4194304
  (5 shorter events, 0.0 us)
